TPU v7x, 256 devices: a whole 4x4x8 slice. The times are simulated.
256 devices in a mesh: section: 4 (over x), tm: 64 (over y, z, core).
Axes of the slice: x: 4, y: 4, z: 8, core: 2. Of those that a mesh axis runs over, the one named last changes fastest.
Arguments:
- signal: bfloat16 [4, 32768, 256], P(None, 'tm'), may hold values from -6 to 6
- skip_cot: bfloat16 [4, 32768, 256], P(None, 'tm'), may hold values from -6 to 6
- res_cot: bfloat16 [4, 32768, 256], P(None, 'tm'), may hold values from -6 to 6
- w_tap: bfloat16 [4, 256, 512], P('section'), may hold values from -0.25 to 0.25
- w_now: bfloat16 [4, 256, 512], P('section'), may hold values from -0.25 to 0.25
- w_res: bfloat16 [4, 256, 256], P('section'), may hold values from -0.375 to 0.375
- w_skip: bfloat16 [4, 256, 256], P('section'), may hold values from -0.375 to 0.375
Outputs:
- skip_total: bfloat16 [4, 32768, 256], P(None, 'tm')
- input_grads: bfloat16 [4, 4, 32768, 256], P('section', None, 'tm')
- grad_tap: float32 [4, 256, 512], P('section')
- grad_now: float32 [4, 256, 512], P('section')
- grad_res: float32 [4, 256, 256], P('section')
- grad_skip: float32 [4, 256, 256], P('section')
All inputs are finite; a program needn't handle non-finite values.
Results may differ from a plain program's by a relative error of at most 0.01.
Values may be sent and summed in bfloat16 or wider, within the bound.
A program may use at most 64 MiB of HBM per device.

v0:
```python
import math

import jax
import jax.numpy as jnp
from jax import lax
from jax.sharding import PartitionSpec as P

SPAN = 4


def passed_along(x, axis, by):
    size = lax.axis_size(axis)
    pairs = [(i, i + by) for i in range(size) if 0 <= i + by < size]
    return lax.ppermute(x, axis, pairs)


def flat_dot(left, right):
    result = jnp.dot(left.reshape(-1, left.shape[-1]), right, preferred_element_type=jnp.float32)
    return result.reshape(left.shape[:-1] + (right.shape[-1],))


def rows_spanning(left, right):
    return lax.dot_general(
        left.reshape(-1, left.shape[-1]),
        right.reshape(-1, right.shape[-1]),
        (((0,), (0,)), ((), ())),
        preferred_element_type=jnp.float32,
    )


def tap_rows(values, chosen, delayed):
    result = jnp.zeros_like(values)
    for layer_number, selected in chosen:
        if delayed:
            arrived = passed_along(values, "tm", SPAN << layer_number)
        else:
            arrived = passed_along(values, "tm", -(SPAN << layer_number))
        result = jnp.where(selected, arrived, result)
    return result


def gate_parts(tapped, layer_in, weights):
    pre = flat_dot(tapped, weights[0]) + flat_dot(layer_in, weights[1])
    half_width = pre.shape[-1] // 2
    return (jnp.tanh(pre[..., :half_width]), jax.nn.sigmoid(pre[..., half_width:]))


def layer_forward(layer_in, weights, chosen):
    tapped = tap_rows(layer_in, chosen, True)
    tanh_part, sigmoid_part = gate_parts(tapped, layer_in, weights)
    gated = (tanh_part * sigmoid_part).astype(jnp.bfloat16)
    stream_out = (layer_in.astype(jnp.float32) + flat_dot(gated, weights[2])).astype(jnp.bfloat16)
    return (tapped, stream_out, flat_dot(gated, weights[3]))


def layer_backward(layer_in, tapped, grad_out, skip_grad, weights, chosen):
    tanh_part, sigmoid_part = gate_parts(tapped, layer_in, weights)
    gated = (tanh_part * sigmoid_part).astype(jnp.bfloat16)
    grad_gated = flat_dot(grad_out, weights[2].T) + flat_dot(skip_grad, weights[3].T)
    grad_pre = jnp.concatenate(
        [
            grad_gated * sigmoid_part * (1.0 - tanh_part * tanh_part),
            grad_gated * tanh_part * sigmoid_part * (1.0 - sigmoid_part),
        ],
        axis=-1,
    ).astype(jnp.bfloat16)
    terms = (
        rows_spanning(tapped, grad_pre),
        rows_spanning(layer_in, grad_pre),
        rows_spanning(gated, grad_out),
        rows_spanning(gated, skip_grad),
    )
    back_term = flat_dot(grad_pre, weights[0].T).astype(jnp.bfloat16)
    arrived = tap_rows(back_term, chosen, False)
    grad_in = (
        grad_out.astype(jnp.float32)
        + flat_dot(grad_pre, weights[1].T)
        + arrived.astype(jnp.float32)
    )
    return (grad_in.astype(jnp.bfloat16), terms)


def run_sequences(signal, skip_cot, res_cot, w_tap, w_now, w_res, w_skip, section_index, sections):
    number = signal.shape[0]
    per_section = number // sections
    every_tap, every_now, every_res, skip_outputs_all = (
        lax.all_gather(w_tap, "section", axis=0, tiled=True),
        lax.all_gather(w_now, "section", axis=0, tiled=True),
        lax.all_gather(w_res, "section", axis=0, tiled=True),
        lax.all_gather(w_skip, "section", axis=0, tiled=True),
    )
    anchor = section_index * per_section
    stream = lax.dynamic_slice_in_dim(signal, anchor, per_section, 0)
    skip_grad = lax.dynamic_slice_in_dim(skip_cot, anchor, per_section, 0)
    grad_out = lax.dynamic_slice_in_dim(res_cot, anchor, per_section, 0)
    skip_running_sum = jnp.zeros(skip_grad.shape, jnp.float32)
    saved_in = []
    saved_tap = []
    for layer_number in range(sections):
        weights = (
            every_tap[layer_number],
            every_now[layer_number],
            every_res[layer_number],
            skip_outputs_all[layer_number],
        )
        tapped, stream_out, skip_term = layer_forward(stream, weights, [(layer_number, True)])
        saved_in.append(stream)
        saved_tap.append(tapped)
        skip_running_sum = skip_running_sum + skip_term
        stream = stream_out
    skip_total = lax.all_gather(
        skip_running_sum.astype(jnp.bfloat16), "section", axis=0, tiled=True
    )
    grad_list = [None] * sections
    term_list = [None] * sections
    for layer_number in reversed(range(sections)):
        weights = (
            every_tap[layer_number],
            every_now[layer_number],
            every_res[layer_number],
            skip_outputs_all[layer_number],
        )
        grad_in, terms = layer_backward(
            saved_in[layer_number],
            saved_tap[layer_number],
            grad_out,
            skip_grad,
            weights,
            [(layer_number, True)],
        )
        grad_list[layer_number] = grad_in
        term_list[layer_number] = terms
        grad_out = grad_in
    stacked = jnp.stack(grad_list)
    input_grads = lax.all_to_all(stacked, "section", split_axis=0, concat_axis=1, tiled=True)[0]
    partial_sums = (
        lax.psum_scatter(
            jnp.stack([term[0] for term in term_list]), "section", scatter_dimension=0, tiled=True
        ),
        lax.psum_scatter(
            jnp.stack([term[1] for term in term_list]), "section", scatter_dimension=0, tiled=True
        ),
        lax.psum_scatter(
            jnp.stack([term[2] for term in term_list]), "section", scatter_dimension=0, tiled=True
        ),
        lax.psum_scatter(
            jnp.stack([term[3] for term in term_list]), "section", scatter_dimension=0, tiled=True
        ),
    )
    return (skip_total, input_grads, tuple(partial_sums))


def body(signal, skip_cot, res_cot, w_tap, w_now, w_res, w_skip):
    sections = lax.axis_size("section")
    shards = lax.axis_size("tm")
    section_index = lax.axis_index("section")
    number, seq_rows, channels = signal.shape
    skip_total, input_grads, partial_sums = run_sequences(
        signal, skip_cot, res_cot, w_tap, w_now, w_res, w_skip, section_index, sections
    )
    summed = lax.psum((partial_sums[0], partial_sums[1], partial_sums[2], partial_sums[3]), "tm")
    grad_scale = 1.0 / math.sqrt(number * seq_rows * shards)
    return (
        skip_total,
        input_grads[None],
        summed[0] * grad_scale,
        summed[1] * grad_scale,
        summed[2] * grad_scale,
        summed[3] * grad_scale,
    )


def solution(mesh):
    in_specs = (
        P(None, "tm", None),
        P(None, "tm", None),
        P(None, "tm", None),
        P("section", None, None),
        P("section", None, None),
        P("section", None, None),
        P("section", None, None),
    )
    out_specs = (
        P(None, "tm", None),
        P("section", None, "tm", None),
        P("section", None, None),
        P("section", None, None),
        P("section", None, None),
        P("section", None, None),
    )
    return jax.shard_map(body, mesh=mesh, in_specs=in_specs, out_specs=out_specs, check_vma=False)
```

profile of v0, /device:TPU:1, one launch (start us, length us, event | category | flops | bytes accessed | tf_op | source)
XLA Modules:
  0.0 490.1 jit_solution(7062506059764534918)
XLA Ops:
  7.2 0.7 all-gather.7.cloned.1.call-update
  8.0 0.7 all-gather.5.cloned.1.call-update
  8.7 1.0 constant_dynamic-slice_fusion
  9.7 5.7 %collective-permute-start = (bf16[1,512,256]{2,1,0:T(8,128)(2,1)S(1)}, bf16[1,512,256]{2,1,0:T(8,128)(2,1)S(1)}, u32[]{:S(2)}, u32[]{:S(2)}) collective-permute-start(bf16[1,512,256]{2,1,0:T(8,128)(2,1)S(1)} %constant_dynamic-slice_fusion), channel_id=1, source_target_pairs={{0,4},{1,5},{2,6},{3,7},{4,8},{5,9},{6,10},{7,11},{8,12},{9,13},{1... | collective-permute-start | bytes 786440 | tf_op jit(solution)/shard_map/ppermute | solution.py:14
  15.4 11.9 %all_gather.18 = bf16[4,256,256]{2,1,0:T(8,128)(2,1)S(1)} all-gather(bf16[1,256,256]{2,1,0:T(8,128)(2,1)} %param.12), channel_id=1, replica_groups=mesh['section'=4,'tm'=64] {'section'}, dimensions={0}, use_global_device_ids=true | all-gather | bytes 655360 | tf_op jit(solution)/shard_map/all_gather | solution.py:89
  27.3 13.3 %all_gather.17 = bf16[4,256,256]{2,1,0:T(8,128)(2,1)S(1)} all-gather(bf16[1,256,256]{2,1,0:T(8,128)(2,1)} %param.13), channel_id=1, replica_groups=mesh['section'=4,'tm'=64] {'section'}, dimensions={0}, use_global_device_ids=true | all-gather | bytes 655360 | tf_op jit(solution)/shard_map/all_gather | solution.py:90
  40.6 2.2 fusion.63
  42.8 1.1 fusion.59
  43.9 1.3 fusion.81
  45.2 23.2 %all-gather.5.cloned.1.call-done = bf16[4,256,512]{2,1,0:T(8,128)(2,1)} async-done(((bf16[1,256,512]{2,1,0:T(8,128)(2,1)}), bf16[4,256,512]{2,1,0:T(8,128)(2,1)}) %all-gather.5.cloned.1.call-update) | async-done | bytes 1048592 | tf_op jit(solution)/shard_map/all_gather | solution.py:87
  68.4 1.3 fusion.3
  70.4 7.5 %collective-permute-start.1 = (bf16[1,512,256]{2,1,0:T(8,128)(2,1)S(1)}, bf16[1,512,256]{2,1,0:T(8,128)(2,1)S(1)}, u32[]{:S(2)}, u32[]{:S(2)}) collective-permute-start(bf16[1,512,256]{2,1,0:T(8,128)(2,1)S(1)} %fusion.14), channel_id=1, source_target_pairs={{0,8},{1,9},{2,10},{3,11},{4,12},{5,13},{6,14},{7,15},{8,16},{9,17... | collective-permute-start | bytes 786440 | tf_op jit(solution)/shard_map/ppermute | solution.py:14
  78.3 3.0 collective-permute-done.1
  81.9 1.3 fusion.13
  83.5 7.1 %collective-permute-start.2 = (bf16[1,512,256]{2,1,0:T(8,128)(2,1)S(1)}, bf16[1,512,256]{2,1,0:T(8,128)(2,1)}, u32[]{:S(2)}, u32[]{:S(2)}) collective-permute-start(bf16[1,512,256]{2,1,0:T(8,128)(2,1)S(1)} %fusion.13), channel_id=1, source_target_pairs={{0,16},{1,17},{2,18},{3,19},{4,20},{5,21},{6,22},{7,23},{8,24},{9,... | collective-permute-start | bytes 786440 | tf_op jit(solution)/shard_map/ppermute | solution.py:14
  90.9 2.2 collective-permute-done.2
  93.2 1.3 fusion.1
  94.7 1.3 fusion.12
  96.3 5.6 %collective-permute-start.3 = (bf16[1,512,256]{2,1,0:T(8,128)(2,1)S(1)}, bf16[1,512,256]{2,1,0:T(8,128)(2,1)S(1)}, u32[]{:S(2)}, u32[]{:S(2)}) collective-permute-start(bf16[1,512,256]{2,1,0:T(8,128)(2,1)S(1)} %fusion.12), channel_id=1, source_target_pairs={{0,32},{1,33},{2,34},{3,35},{4,36},{5,37},{6,38},{7,39},{8,40},{9,... | collective-permute-start | bytes 786440 | tf_op jit(solution)/shard_map/ppermute | solution.py:14
  102.2 2.9 collective-permute-done.3
  105.5 0.5 fusion.36
  106.0 1.1 fusion.16
  107.1 1.3 collective-permute-start.4
  108.7 1.1 pad_maximum_fusion.4
  109.8 6.2 %collective-permute-done.4 = bf16[1,512,256]{2,1,0:T(8,128)(2,1)} collective-permute-done((bf16[1,512,256]{2,1,0:T(8,128)(2,1)}, bf16[1,512,256]{2,1,0:T(8,128)(2,1)}, u32[]{:S(2)}, u32[]{:S(2)}) %collective-permute-start.4) | collective-permute-done | bytes 262176 | tf_op jit(solution)/shard_map/ppermute | solution.py:14
  116.0 1.6 add_convert_fusion.3
  117.7 1.9 fusion.38
  119.6 0.3 fusion.17
  120.0 1.4 collective-permute-start.5
  121.7 1.2 convolution_bitcast_fusion.19
  122.9 4.3 collective-permute-done.5
  127.3 0.3 add_convert_fusion.2
  127.7 1.4 fusion.40
  129.1 0.3 fusion.18
  129.5 1.3 collective-permute-start.6
  131.2 9.2 %collective-permute-done.6 = bf16[1,512,256]{2,1,0:T(8,128)(2,1)S(1)} collective-permute-done((bf16[1,512,256]{2,1,0:T(8,128)(2,1)S(1)}, bf16[1,512,256]{2,1,0:T(8,128)(2,1)S(1)}, u32[]{:S(2)}, u32[]{:S(2)}) %collective-permute-start.6) | collective-permute-done | bytes 262176 | tf_op jit(solution)/shard_map/ppermute | solution.py:14
  140.5 0.3 add_convert_fusion.1
  141.1 0.5 copy-done.42
  141.6 1.0 pad_maximum_fusion.3
  143.0 1.5 convolution_bitcast_fusion
  144.5 0.3 convolution_bitcast_fusion.1
  144.9 0.3 convolution_bitcast_fusion.2
  145.3 1.3 fusion.42
  146.6 0.7 copy-done.25
  147.8 1.5 pad_maximum_fusion.1
  149.6 1.5 convolution_bitcast_fusion.4
  151.1 1.5 convolution_bitcast_fusion.5
  152.6 1.4 convolution_bitcast_fusion.6
  154.3 1.5 pad_maximum_fusion
  156.8 1.0 fusion.15
  157.9 1.4 fusion.19
  159.2 1.3 collective-permute-start.7
  160.5 18.2 %collective-permute-done.7 = bf16[1,512,256]{2,1,0:T(8,128)(2,1)S(1)} collective-permute-done((bf16[1,512,256]{2,1,0:T(8,128)(2,1)S(1)}, bf16[1,512,256]{2,1,0:T(8,128)(2,1)S(1)}, u32[]{:S(2)}, u32[]{:S(2)}) %collective-permute-start.7) | collective-permute-done | bytes 262176 | tf_op jit(solution)/shard_map/ppermute | solution.py:14
  178.7 1.4 fusion.44
  180.2 1.1 pad_maximum_fusion.2
  181.3 3.5 all-to-all-start
  184.9 34.8 %reduce-scatter.7.cloned.1.call-done = f32[1,256,512]{2,1,0:T(8,128)} async-done(((f32[4,256,512]{2,1,0:T(8,128)}), f32[1,256,512]{2,1,0:T(8,128)}) %reduce-scatter.7.cloned.1.call-update) | async-done | bytes 524304 | tf_op jit(solution)/shard_map/reduce_scatter | solution.py:140
  219.7 36.6 %reduce-scatter.5.cloned.1.call-done = f32[1,256,512]{2,1,0:T(8,128)} async-done(((f32[4,256,512]{2,1,0:T(8,128)}), f32[1,256,512]{2,1,0:T(8,128)}) %reduce-scatter.5.cloned.1.call-update) | async-done | bytes 524304 | tf_op jit(solution)/shard_map/reduce_scatter | solution.py:137
  256.4 26.8 %all-gather.9.cloned.1.call-done = bf16[2048,256]{1,0:T(8,128)(2,1)} async-done(((bf16[512,256]{1,0:T(8,128)(2,1)}), bf16[2048,256]{1,0:T(8,128)(2,1)}) %all-gather.9.cloned.1.call-update) | async-done | bytes 1048592 | tf_op jit(solution)/shard_map/all_gather | solution.py:111
  283.2 194.0 %all-reduce.3.cloned.1.call-done = (f32[1,256,512]{2,1,0:T(8,128)}, f32[1,256,512]{2,1,0:T(8,128)}, f32[1,256,256]{2,1,0:T(8,128)}, f32[1,256,256]{2,1,0:T(8,128)}) async-done(((f32[1,256,512]{2,1,0:T(8,128)}, f32[1,256,512]{2,1,0:T(8,128)}, f32[1,256,256]{2,1,0:T(8,128)}, f32[1,256,256]{2,1,0:T(8,128)}), (f32[1,256,512]{2,1,0:T(8,128)}, f32[1,256,512]{2,1,0:T(8,128)}, f32[1,256,256]{2,1,0:T(8,128)}, ...) | async-done | bytes 1572880 | tf_op jit(solution)/shard_map/psum | solution.py:161
  477.2 1.9 broadcast_multiply_fusion.2
  479.1 2.3 broadcast_multiply_fusion
  481.3 1.0 copy.19
  482.3 1.0 copy.20
  (132 shorter events, 7.2 us)
Async XLA Ops:
  7.2 35.6 %copy-start = (bf16[4,512,256]{2,1,0:T(8,128)(2,1)S(1)}, bf16[4,512,256]{2,1,0:T(8,128)(2,1)}, u32[]{:S(2)}) copy-start(bf16[4,512,256]{2,1,0:T(8,128)(2,1)} %param.8) | copy-start | bytes 3145732
  7.2 36.7 %all-gather.7.cloned.1.call-start = ((), (), s32[]{:S(2)}) async-start(), calls=%async_computation.6 | async-start | bytes 1310720 | tf_op jit(solution)/shard_map/all_gather | solution.py:88
  7.9 60.5 %all-gather.5.cloned.1.call-start = ((), (), s32[]{:S(2)}) async-start(), calls=%async_computation.5 | async-start | bytes 1310720 | tf_op jit(solution)/shard_map/all_gather | solution.py:87
  8.7 176.2 %reduce-scatter.11.cloned.1.call-start = ((), (), s32[]{:S(2)}) async-start(), calls=%async_computation.10 | async-start | bytes 1310720 | tf_op jit(solution)/shard_map/reduce_scatter | solution.py:146
  9.7 35.5 %collective-permute-start = (bf16[1,512,256]{2,1,0:T(8,128)(2,1)S(1)}, bf16[1,512,256]{2,1,0:T(8,128)(2,1)S(1)}, u32[]{:S(2)}, u32[]{:S(2)}) collective-permute-start(bf16[1,512,256]{2,1,0:T(8,128)(2,1)S(1)} %constant_dynamic-slice_fusion), channel_id=1, source_target_pairs={{0,4},{1,5},{2,6},{3,7},{4,8},{5,9},{6,10},{7,11},{8,12},{9,13},{1... | collective-permute-start | bytes 786440 | tf_op jit(solution)/shard_map/ppermute | solution.py:14
  27.3 54.1 %copy-start.11 = (bf16[4,256,256]{2,1,0:T(8,128)(2,1)}, bf16[4,256,256]{2,1,0:T(8,128)(2,1)S(1)}, u32[]{:S(2)}) copy-start(bf16[4,256,256]{2,1,0:T(8,128)(2,1)S(1)} %all_gather.18) | copy-start | bytes 1572868
  40.6 2.2 copy-start.6
  45.2 23.2 %copy-start.14 = (bf16[1,512,256]{2,1,0:T(8,128)(2,1)}, bf16[1,512,256]{2,1,0:T(8,128)(2,1)S(1)}, u32[]{:S(2)}) copy-start(bf16[1,512,256]{2,1,0:T(8,128)(2,1)S(1)} %collective-permute-done) | copy-start | bytes 786436
  69.7 8.6 %copy-start.1 = (f32[1,512,512]{1,2,0:T(8,128)}, f32[1,512,512]{1,2,0:T(8,128)S(1)}, u32[]{:S(2)}) copy-start(f32[1,512,512]{1,2,0:T(8,128)S(1)} %fusion.3) | copy-start | bytes 3145732
  69.7 8.3 %copy-start.36 = (bf16[4,256,512]{2,1,0:T(8,128)(2,1)S(1)}, bf16[4,256,512]{2,1,0:T(8,128)(2,1)}, u32[]{:S(2)}) copy-start(bf16[4,256,512]{2,1,0:T(8,128)(2,1)} %all-gather.7.cloned.1.call-done) | copy-start | bytes 3145732
  69.7 11.6 %copy-start.12 = (bf16[4,256,512]{2,1,0:T(8,128)(2,1)S(1)}, bf16[4,256,512]{2,1,0:T(8,128)(2,1)}, u32[]{:S(2)}) copy-start(bf16[4,256,512]{2,1,0:T(8,128)(2,1)} %all-gather.5.cloned.1.call-done) | copy-start | bytes 3145732
  70.4 10.9 %collective-permute-start.1 = (bf16[1,512,256]{2,1,0:T(8,128)(2,1)S(1)}, bf16[1,512,256]{2,1,0:T(8,128)(2,1)S(1)}, u32[]{:S(2)}, u32[]{:S(2)}) collective-permute-start(bf16[1,512,256]{2,1,0:T(8,128)(2,1)S(1)} %fusion.14), channel_id=1, source_target_pairs={{0,8},{1,9},{2,10},{3,11},{4,12},{5,13},{6,14},{7,15},{8,16},{9,17... | collective-permute-start | bytes 786440 | tf_op jit(solution)/shard_map/ppermute | solution.py:14
  81.3 1.9 copy-start.16
  81.7 9.2 %copy-start.3 = (f32[1,512,512]{1,2,0:T(8,128)}, f32[1,512,512]{1,2,0:T(8,128)S(1)}, u32[]{:S(2)}) copy-start(f32[1,512,512]{1,2,0:T(8,128)S(1)} %fusion.2) | copy-start | bytes 3145732
  83.5 9.6 %collective-permute-start.2 = (bf16[1,512,256]{2,1,0:T(8,128)(2,1)S(1)}, bf16[1,512,256]{2,1,0:T(8,128)(2,1)}, u32[]{:S(2)}, u32[]{:S(2)}) collective-permute-start(bf16[1,512,256]{2,1,0:T(8,128)(2,1)S(1)} %fusion.13), channel_id=1, source_target_pairs={{0,16},{1,17},{2,18},{3,19},{4,20},{5,21},{6,22},{7,23},{8,24},{9,... | collective-permute-start | bytes 786440 | tf_op jit(solution)/shard_map/ppermute | solution.py:14
  94.4 7.8 %copy-start.5 = (f32[1,512,512]{1,2,0:T(8,128)}, f32[1,512,512]{1,2,0:T(8,128)S(1)}, u32[]{:S(2)}) copy-start(f32[1,512,512]{1,2,0:T(8,128)S(1)} %fusion.1) | copy-start | bytes 3145732
  96.2 9.3 %copy-start.7 = (bf16[4,256,256]{2,1,0:T(8,128)(2,1)S(1)}, bf16[4,256,256]{2,1,0:T(8,128)(2,1)}, u32[]{:S(2)}) copy-start(bf16[4,256,256]{2,1,0:T(8,128)(2,1)} %copy-done.6) | copy-start | bytes 1572868
  96.3 9.3 %copy-start.45 = (f32[512,256]{0,1:T(8,128)S(1)}, f32[512,256]{0,1:T(8,128)}, u32[]{:S(2)}) copy-start(f32[512,256]{0,1:T(8,128)} %fusion.63) | copy-start | bytes 1572868
  96.3 8.9 %collective-permute-start.3 = (bf16[1,512,256]{2,1,0:T(8,128)(2,1)S(1)}, bf16[1,512,256]{2,1,0:T(8,128)(2,1)S(1)}, u32[]{:S(2)}, u32[]{:S(2)}) collective-permute-start(bf16[1,512,256]{2,1,0:T(8,128)(2,1)S(1)} %fusion.12), channel_id=1, source_target_pairs={{0,32},{1,33},{2,34},{3,35},{4,36},{5,37},{6,38},{7,39},{8,40},{9,... | collective-permute-start | bytes 786440 | tf_op jit(solution)/shard_map/ppermute | solution.py:14
  105.2 0.8 copy-start.18
  106.0 2.4 copy-start.8
  106.0 2.6 copy-start.19
  106.0 2.6 copy-start.20
  107.1 8.9 %collective-permute-start.4 = (bf16[1,512,256]{2,1,0:T(8,128)(2,1)}, bf16[1,512,256]{2,1,0:T(8,128)(2,1)}, u32[]{:S(2)}, u32[]{:S(2)}) collective-permute-start(bf16[1,512,256]{2,1,0:T(8,128)(2,1)} %fusion.16), channel_id=1, source_target_pairs={{32,0},{33,1},{34,2},{35,3},{36,4},{37,5},{38,6},{39,7},{40,8},{41... | collective-permute-start | bytes 786440 | tf_op jit(solution)/shard_map/ppermute | solution.py:14
  109.8 75.1 %reduce-scatter.9.cloned.1.call-start = ((), (), s32[]{:S(2)}) async-start(), calls=%async_computation.9 | async-start | bytes 1310720 | tf_op jit(solution)/shard_map/reduce_scatter | solution.py:143
  117.6 13.1 %copy-start.38 = (bf16[1,512,256]{2,1,0:T(8,128)(2,1)}, bf16[1,512,256]{2,1,0:T(8,128)(2,1)S(1)}, u32[]{:S(2)}) copy-start(bf16[1,512,256]{2,1,0:T(8,128)(2,1)S(1)} %add_convert_fusion.3) | copy-start | bytes 786436
  117.6 2.0 copy-start.13
  119.6 8.0 %copy-start.21 = (bf16[512,256]{0,1:T(8,128)(2,1)}, bf16[512,256]{0,1:T(8,128)(2,1)S(1)}, u32[]{:S(2)}) copy-start(bf16[512,256]{0,1:T(8,128)(2,1)S(1)} %get-tuple-element.14) | copy-start | bytes 786436
  119.6 8.0 %copy-start.23 = (bf16[512,256]{0,1:T(8,128)(2,1)}, bf16[512,256]{0,1:T(8,128)(2,1)S(1)}, u32[]{:S(2)}) copy-start(bf16[512,256]{0,1:T(8,128)(2,1)S(1)} %get-tuple-element.15) | copy-start | bytes 786436
  119.6 2.1 copy-start.9
  119.6 7.6 %copy-start.37 = (bf16[4,256,512]{2,1,0:T(8,128)(2,1)S(1)}, bf16[4,256,512]{2,1,0:T(8,128)(2,1)}, u32[]{:S(2)}) copy-start(bf16[4,256,512]{2,1,0:T(8,128)(2,1)} %all-gather.7.cloned.1.call-done) | copy-start | bytes 3145732
  120.0 7.6 %copy-start.4 = (f32[1,512,512]{1,2,0:T(8,128)S(1)}, f32[1,512,512]{1,2,0:T(8,128)}, u32[]{:S(2)}) copy-start(f32[1,512,512]{1,2,0:T(8,128)} %copy-done.3) | copy-start | bytes 3145732
  120.0 7.2 %collective-permute-start.5 = (bf16[1,512,256]{2,1,0:T(8,128)(2,1)S(1)}, bf16[1,512,256]{2,1,0:T(8,128)(2,1)S(1)}, u32[]{:S(2)}, u32[]{:S(2)}) collective-permute-start(bf16[1,512,256]{2,1,0:T(8,128)(2,1)S(1)} %fusion.17), channel_id=1, source_target_pairs={{16,0},{17,1},{18,2},{19,3},{20,4},{21,5},{22,6},{23,7},{24,8},{25... | collective-permute-start | bytes 786440 | tf_op jit(solution)/shard_map/ppermute | solution.py:14
  127.6 12.8 %copy-start.40 = (bf16[1,512,256]{2,1,0:T(8,128)(2,1)}, bf16[1,512,256]{2,1,0:T(8,128)(2,1)S(1)}, u32[]{:S(2)}) copy-start(bf16[1,512,256]{2,1,0:T(8,128)(2,1)S(1)} %add_convert_fusion.2) | copy-start | bytes 786436
  129.1 11.8 %copy-start.31 = (bf16[512,256]{0,1:T(8,128)(2,1)}, bf16[512,256]{0,1:T(8,128)(2,1)S(1)}, u32[]{:S(2)}) copy-start(bf16[512,256]{0,1:T(8,128)(2,1)S(1)} %get-tuple-element.12) | copy-start | bytes 786436
  129.1 11.8 %copy-start.33 = (bf16[512,256]{0,1:T(8,128)(2,1)}, bf16[512,256]{0,1:T(8,128)(2,1)S(1)}, u32[]{:S(2)}) copy-start(bf16[512,256]{0,1:T(8,128)(2,1)S(1)} %get-tuple-element.13) | copy-start | bytes 786436
  129.5 11.0 %collective-permute-start.6 = (bf16[1,512,256]{2,1,0:T(8,128)(2,1)S(1)}, bf16[1,512,256]{2,1,0:T(8,128)(2,1)S(1)}, u32[]{:S(2)}, u32[]{:S(2)}) collective-permute-start(bf16[1,512,256]{2,1,0:T(8,128)(2,1)S(1)} %fusion.18), channel_id=1, source_target_pairs={{8,0},{9,1},{10,2},{11,3},{12,4},{13,5},{14,6},{15,7},{16,8},{17,9... | collective-permute-start | bytes 786440 | tf_op jit(solution)/shard_map/ppermute | solution.py:14
  140.9 0.7 copy-start.42
  142.6 77.1 %reduce-scatter.7.cloned.1.call-start = ((), (), s32[]{:S(2)}) async-start(), calls=%async_computation.8 | async-start | bytes 2621440 | tf_op jit(solution)/shard_map/reduce_scatter | solution.py:140
  142.7 1.8 copy-start.22
  142.7 1.8 copy-start.24
  142.7 2.2 copy-start.32
  142.7 2.2 copy-start.34
  143.0 2.3 copy-start.2
  143.0 2.3 copy-start.43
  146.6 0.7 copy-start.25
  146.6 0.8 copy-start.28
  149.3 3.3 copy-start.17
  149.3 4.6 copy-start.15
  149.3 107.0 %reduce-scatter.5.cloned.1.call-start = ((), (), s32[]{:S(2)}) async-start(), calls=%async_computation.7 | async-start | bytes 2621440 | tf_op jit(solution)/shard_map/reduce_scatter | solution.py:137
  149.5 4.4 copy-start.26
  149.6 4.4 copy-start.29
  155.9 1.0 copy-start.10
  155.9 127.3 %all-gather.9.cloned.1.call-start = ((), (), s32[]{:S(2)}) async-start(), calls=%async_computation.11 | async-start | bytes 1310720 | tf_op jit(solution)/shard_map/all_gather | solution.py:111
  156.2 1.6 copy-start.27
  156.2 1.6 copy-start.30
  157.8 22.3 %copy-start.39 = (bf16[1,512,256]{2,1,0:T(8,128)(2,1)S(1)}, bf16[1,512,256]{2,1,0:T(8,128)(2,1)}, u32[]{:S(2)}) copy-start(bf16[1,512,256]{2,1,0:T(8,128)(2,1)} %copy-done.38) | copy-start | bytes 786436
  157.8 22.3 %copy-start.41 = (bf16[1,512,256]{2,1,0:T(8,128)(2,1)S(1)}, bf16[1,512,256]{2,1,0:T(8,128)(2,1)}, u32[]{:S(2)}) copy-start(bf16[1,512,256]{2,1,0:T(8,128)(2,1)} %copy-done.40) | copy-start | bytes 786436
  157.8 22.3 %copy-start.44 = (bf16[1,512,256]{2,1,0:T(8,128)(2,1)S(1)}, bf16[1,512,256]{2,1,0:T(8,128)(2,1)}, u32[]{:S(2)}) copy-start(bf16[1,512,256]{2,1,0:T(8,128)(2,1)} %copy-done.42) | copy-start | bytes 786436
  159.2 19.5 %collective-permute-start.7 = (bf16[1,512,256]{2,1,0:T(8,128)(2,1)S(1)}, bf16[1,512,256]{2,1,0:T(8,128)(2,1)S(1)}, u32[]{:S(2)}, u32[]{:S(2)}) collective-permute-start(bf16[1,512,256]{2,1,0:T(8,128)(2,1)S(1)} %fusion.19), channel_id=1, source_target_pairs={{4,0},{5,1},{6,2},{7,3},{8,4},{9,5},{10,6},{11,7},{12,8},{13,9},{1... | collective-permute-start | bytes 786440 | tf_op jit(solution)/shard_map/ppermute | solution.py:14
  181.3 101.9 %all-to-all-start = ((bf16[4,1,512,256]{3,2,1,0:T(8,128)(2,1)}), bf16[4,1,512,256]{3,2,1,0:T(8,128)(2,1)S(1)}, u32[]{:S(2)}, u32[]{:S(2)}) async-start(bf16[4,1,512,256]{3,2,1,0:T(8,128)(2,1)} %pad_maximum_fusion.2), calls=%async_computation | async-start | bytes 2097152 | tf_op jit(solution)/shard_map/all_to_all | solution.py:135
  184.8 292.4 %all-reduce.3.cloned.1.call-start = ((), (), s32[]{:S(2)}) async-start(), calls=%async_computation.12 | async-start | bytes 3145728 | tf_op jit(solution)/shard_map/psum | solution.py:161
  283.2 198.2 %copy-start.35 = (bf16[2048,256]{1,0:T(8,128)(2,1)S(1)}, bf16[2048,256]{1,0:T(8,128)(2,1)}, u32[]{:S(2)}) copy-start(bf16[2048,256]{1,0:T(8,128)(2,1)} %all-gather.9.cloned.1.call-done) | copy-start | bytes 3145732
Sparse Core Ops, SparseCore 0:
  9.8 31.2 all-gather.6
  42.9 25.4 all-gather.4
  109.9 36.3 reduce-scatter.10
  149.3 32.3 reduce-scatter.8
  184.1 35.6 reduce-scatter.6
  222.1 34.1 reduce-scatter.4
  258.7 24.3 all-gather.8
  286.8 190.3 all-reduce.2
where the time goes:
time: 492 us; the launch traced here: 490 us
  waiting for transfers between devices  363 us (74%)
  matrix products  35.9 us (7%)
  starting transfers between devices  35.2 us (7%)
  blocking collectives  25.2 us (5%)
  between operations  15.1 us (3%)
  other arithmetic  11.1 us (2%)
    psum x1, waiting for transfers between devices, body(): lax.psum((partial_sums[0], partial_sums[1], partial_sums[2], partial_sums...  194 us
    ppermute x8, waiting for transfers between devices, passed_along(): return lax.ppermute(x, axis, pairs)  46.2 us
    reduce_scatter x1, waiting for transfers between devices, run_sequences(): lax.psum_scatter(jnp.stack([term[0] for term in term_list]), 'section', s...  36.6 us
    reduce_scatter x1, waiting for transfers between devices, run_sequences(): lax.psum_scatter(jnp.stack([term[1] for term in term_list]), 'section', s...  34.8 us
    ppermute x8, starting transfers between devices, passed_along(): return lax.ppermute(x, axis, pairs)  31.2 us
    all_gather x1, waiting for transfers between devices, run_sequences(): lax.all_gather(skip_running_sum.astype(jnp.bfloat16), 'section', axis=0,...  26.8 us
    dot_general x31, matrix products, flat_dot(): jnp.dot(left.reshape(-1, left.shape[-1]), right, preferred_element_type=j...  25.9 us
    all_gather x1, waiting for transfers between devices, run_sequences(): lax.all_gather(w_tap, 'section', axis=0, tiled=True)  23.2 us
  transfers between devices with their start and end apart: 17, of which 12 were waited for; matrix products, arithmetic and copies ran while one was open for 7% of the time, Pallas kernels for 0%

commit v1 on v0

v1 whole, which is shorter than its diff:
```python
import math

import jax
import jax.numpy as jnp
from jax import lax
from jax.experimental import pallas as pl
from jax.experimental.pallas import tpu as pltpu
from jax.sharding import PartitionSpec as P

MESH = pl.DeviceIdType.MESH
BF = jnp.bfloat16
F32 = jnp.float32

SECTIONS = 4
YS, ZS, CORES = 4, 8, 2
SHARDS = YS * ZS * CORES
SPAN = 4
ROWS, CH = 512, 256
PARTS = 2
PART = ROWS // PARTS
HALF_ROWS = 384
PIECE = HALF_ROWS // ZS
LANES = 128


def dot(a, b):
    return jnp.dot(a, b, preferred_element_type=F32)


def dot_bt(a, b):
    return lax.dot_general(a, b, (((1,), (1,)), ((), ())), preferred_element_type=F32)


def dot_at(a, b):
    return lax.dot_general(a, b, (((0,), (0,)), ((), ())), preferred_element_type=F32)


def kernel(
    signal, skip_cot, res_cot, w_tap, w_now, w_res, w_skip,
    out_skip, out_grads, out_sums,
    wts, th, act, sig, gated_s, skip_acc, skip_out, cot, grad, dz, back_s, back_r, part_g,
    sums, pair_r, pair_s, y_r, y_s, z_r, z_s, x_r, full,
    sem_in, sem_loc, w_ss, w_rs, wp_ss, wp_rs, tap_ss, tap_rs, back_ss, back_rs,
    skip_ss, skip_rs, ig_ss, ig_rs, s1_ss, s1_rs, s2_ss, s2_rs, s3_ss, s3_rs,
    s4_ss, s4_rs, s5_ss, s5_rs, s6_ss, s6_rs, s7_ss, s7_rs,
):
    x = lax.axis_index("section")
    t = lax.axis_index("tm")
    core = lax.rem(t, CORES)
    z = lax.rem(t // CORES, ZS)
    y = t // (CORES * ZS)
    mate = t + 1 - 2 * core

    def at_x(j):
        return lax.rem(x + j + SECTIONS, SECTIONS)

    def at_y(j):
        return (lax.rem(y + j + YS, YS) * ZS + z) * CORES + core

    def at_z(j):
        return (y * ZS + lax.rem(z + j + ZS, ZS)) * CORES + core

    def rows(c):
        return pl.ds(c * PART, PART)

    def remote(src, dst, ss, rs, to_x, to_t):
        return pltpu.make_async_remote_copy(
            src_ref=src, dst_ref=dst, send_sem=ss, recv_sem=rs,
            device_id=(to_x, to_t), device_id_type=MESH,
        )

    def w_copy(layer, j):
        half = pl.ds(core * HALF_ROWS, HALF_ROWS)
        return remote(
            wts.at[layer, half], wts.at[layer, half],
            w_ss.at[j - 1], w_rs.at[j - 1], at_x(j), t,
        )

    def w_recv(layer):
        j = lax.rem(x - layer + SECTIONS, SECTIONS)
        half = pl.ds(core * HALF_ROWS, HALF_ROWS)
        return remote(
            wts.at[layer, half], wts.at[layer, half],
            w_ss.at[j - 1], w_rs.at[j - 1], layer, t,
        )

    def w_mate(layer, whose):
        half = pl.ds(whose * HALF_ROWS, HALF_ROWS)
        return remote(
            wts.at[layer, half], wts.at[layer, half],
            wp_ss.at[layer], wp_rs.at[layer], x, mate,
        )

    def tap_copy(layer, c, to_t):
        return remote(
            th.at[layer, rows(c), pl.ds(CH, CH)], th.at[layer, rows(c), pl.ds(0, CH)],
            tap_ss.at[layer * PARTS + c], tap_rs.at[layer * PARTS + c], x, to_t,
        )

    def tap_first(c, to_t):
        return remote(
            signal.at[x, rows(c)], th.at[0, rows(c), pl.ds(0, CH)],
            tap_ss.at[c], tap_rs.at[c], x, to_t,
        )

    def back_copy(layer, c, to_t):
        return remote(
            back_s.at[layer, rows(c)], back_r.at[layer, rows(c)],
            back_ss.at[layer * PARTS + c], back_rs.at[layer * PARTS + c], x, to_t,
        )

    def skip_copy(j):
        return remote(
            skip_out, out_skip.at[x], skip_ss.at[j - 1], skip_rs.at[j - 1], at_x(j), t
        )

    def skip_recv(j):
        return remote(
            skip_out, out_skip.at[at_x(-j)], skip_ss.at[j - 1], skip_rs.at[j - 1], at_x(-j), t
        )

    def ig_copy(layer, c):
        j = lax.rem(layer - x + SECTIONS, SECTIONS)
        return remote(
            grad.at[layer, rows(c)], out_grads.at[0, x, rows(c)],
            ig_ss.at[layer * PARTS + c], ig_rs.at[(j - 1) * PARTS + c], layer, t,
        )

    def ig_recv(j, c):
        return remote(
            grad.at[0, rows(c)], out_grads.at[0, at_x(-j), rows(c)],
            ig_ss.at[c], ig_rs.at[(j - 1) * PARTS + c], at_x(-j), t,
        )

    def ig_own(layer, c):
        return pltpu.make_async_copy(
            grad.at[layer, rows(c)], out_grads.at[0, x, rows(c)], sem_loc.at[c]
        )

    def s1(layer):
        return remote(
            sums.at[layer, 1 - core], pair_r.at[layer],
            s1_ss.at[layer], s1_rs.at[layer], x, mate,
        )

    def s2(layer, j):
        return remote(
            pair_s.at[layer, lax.rem(y + j, YS)], y_r.at[layer, j - 1],
            s2_ss.at[layer * 3 + j - 1], s2_rs.at[layer * 3 + j - 1], x, at_y(j),
        )

    def piece(i):
        return pl.ds(pl.multiple_of(i * PIECE, 16), PIECE)

    def s3(layer, j):
        return remote(
            y_s.at[layer, piece(lax.rem(z + j, ZS))], z_r.at[layer, j - 1],
            s3_ss.at[layer * 7 + j - 1], s3_rs.at[layer * 7 + j - 1], x, at_z(j),
        )

    def s4(layer):
        j = lax.rem(layer - x + SECTIONS, SECTIONS)
        return remote(
            z_s.at[layer], x_r.at[j - 1], s4_ss.at[layer], s4_rs.at[j - 1], layer, t
        )

    def s4_recv(j):
        return remote(z_s.at[0], x_r.at[j - 1], s4_ss.at[0], s4_rs.at[j - 1], at_x(-j), t)

    def s5(j, whose):
        return remote(
            full.at[core, y, piece(whose)], full.at[core, y, piece(whose)],
            s5_ss.at[j - 1], s5_rs.at[j - 1], x, at_z(j),
        )

    def s6(j, whose):
        return remote(
            full.at[core, whose], full.at[core, whose],
            s6_ss.at[j - 1], s6_rs.at[j - 1], x, at_y(j),
        )

    def s7(whose):
        return remote(full.at[whose], full.at[whose], s7_ss.at[0], s7_rs.at[0], x, mate)

    loads = [
        pltpu.make_async_copy(w_tap.at[0], wts.at[x, pl.ds(0, CH)], sem_in.at[0]),
        pltpu.make_async_copy(w_now.at[0], wts.at[x, pl.ds(CH, CH)], sem_in.at[1]),
        pltpu.make_async_copy(
            w_res.at[0], wts.at[x, pl.ds(2 * CH, CH), pl.ds(0, CH)], sem_in.at[2]
        ),
        pltpu.make_async_copy(
            w_skip.at[0], wts.at[x, pl.ds(2 * CH, CH), pl.ds(CH, CH)], sem_in.at[3]
        ),
        pltpu.make_async_copy(signal.at[x], th.at[0, :, pl.ds(CH, CH)], sem_in.at[4]),
        pltpu.make_async_copy(skip_cot.at[x], cot, sem_in.at[5]),
        pltpu.make_async_copy(res_cot.at[x], grad.at[SECTIONS], sem_in.at[6]),
    ]
    for load in loads:
        load.start()

    barrier = pltpu.get_barrier_semaphore()
    peers = [(at_x(j), t) for j in range(1, SECTIONS)] + [(x, mate)]
    peers += [(x, at_y(j)) for j in range(1, YS)] + [(x, at_z(j)) for j in range(1, ZS)]
    peers += [(x, lax.rem(t + d + SHARDS, SHARDS)) for d in (SPAN, -SPAN, 2 * SPAN, -2 * SPAN)]
    for peer in peers:
        pl.semaphore_signal(barrier, inc=1, device_id=peer, device_id_type=MESH)
    pl.semaphore_wait(barrier, len(peers))

    @pl.when(t + SPAN < SHARDS)
    def _():
        for c in range(PARTS):
            tap_first(c, t + SPAN).start()

    for load in loads[:4]:
        load.wait()
    for j in range(1, SECTIONS):
        w_copy(x, j).start()

    for layer in range(SECTIONS):
        d = SPAN << layer

        @pl.when(t < d)
        def _(layer=layer):
            th[layer, :, pl.ds(0, CH)] = jnp.zeros((ROWS, CH), BF)

        @pl.when(t + d >= SHARDS)
        def _(layer=layer):
            back_r[layer] = jnp.zeros((ROWS, CH), BF)

    skip_acc[...] = jnp.zeros((ROWS, CH), F32)
    for load in loads[4:]:
        load.wait()

    def w_forward(layer):
        @pl.when(x != layer)
        def _():
            w_recv(layer).wait_recv()
            w_mate(layer, core).start()

    w_forward(0)

    def forward(k, d):
        @pl.when(x != k)
        def _():
            w_mate(k, 1 - core).wait_recv()

        for c in range(PARTS):
            @pl.when(t >= d)
            def _():
                tap_copy(k, c, t).wait_recv()

            pre = dot(th[k, rows(c), :], wts[k, pl.ds(0, 2 * CH), :])
            a = jnp.tanh(pre[:, :CH])
            s = jax.nn.sigmoid(pre[:, CH:])
            act[k, rows(c), :] = a
            sig[k, rows(c), :] = s
            gated = (a * s).astype(BF)
            gated_s[k, rows(c), :] = gated
            out = dot(gated, wts[k, pl.ds(2 * CH, CH), :])
            skip_acc[rows(c), :] += out[:, CH:]
            h = th[k, rows(c), pl.ds(CH, CH)].astype(F32)
            th[k + 1, rows(c), pl.ds(CH, CH)] = (h + out[:, :CH]).astype(BF)

            @pl.when(jnp.logical_and(k < SECTIONS - 1, t + 2 * d < SHARDS))
            def _():
                tap_copy(k + 1, c, t + 2 * d).start()

        @pl.when(k < SECTIONS - 1)
        def _():
            w_forward(k + 1)

        return d * 2

    lax.fori_loop(0, SECTIONS, forward, jnp.int32(SPAN))

    skip_out[...] = skip_acc[...].astype(BF)
    for j in range(1, SECTIONS):
        skip_copy(j).start()
    skip_own = pltpu.make_async_copy(skip_out, out_skip.at[x], sem_loc.at[2])
    skip_own.start()

    def s1_to_s2(layer):
        s1(layer).wait_recv()
        pair_s[layer] = (
            sums[layer, core].astype(F32) + pair_r[layer].astype(F32)
        ).astype(BF)
        for j in range(1, YS):
            s2(layer, j).start()

    def s2_to_s3(layer):
        total = pair_s[layer, y].astype(F32)
        for j in range(1, YS):
            s2(layer, j).wait_recv()
            total = total + y_r[layer, j - 1].astype(F32)
        y_s[layer] = total.astype(BF)
        for j in range(1, ZS):
            s3(layer, j).start()

    def s3_to_s4(layer):
        total = y_s[layer, piece(z), :].astype(F32)
        for j in range(1, ZS):
            s3(layer, j).wait_recv()
            total = total + z_r[layer, j - 1].astype(F32)
        z_s[layer] = total.astype(BF)

        @pl.when(x != layer)
        def _():
            s4(layer).start()

    def finish_grad(layer, d, c):
        @pl.when(t + d < SHARDS)
        def _():
            back_copy(layer, c, t).wait_recv()

        g = (part_g[rows(c), :] + back_r[layer, rows(c), :].astype(F32)).astype(BF)
        grad[layer, rows(c), :] = g

        @pl.when(x != layer)
        def _():
            ig_copy(layer, c).start()

        @pl.when(x == layer)
        def _():
            ig_own(layer, c).start()

    def backward(i, d):
        k = SECTIONS - 1 - i
        for c in range(PARTS):
            @pl.when(i > 0)
            def _():
                finish_grad(k + 1, 2 * d, c)

            g = grad[k + 1, rows(c), :]
            du = dot_bt(g, wts[k, pl.ds(2 * CH, CH), pl.ds(0, CH)]) + dot_bt(
                cot[rows(c), :], wts[k, pl.ds(2 * CH, CH), pl.ds(CH, CH)]
            )
            a = act[k, rows(c), :]
            s = sig[k, rows(c), :]
            us = du * s
            dz[rows(c), pl.ds(0, CH)] = (us * (1.0 - a * a)).astype(BF)
            dz[rows(c), pl.ds(CH, CH)] = (us * a * (1.0 - s)).astype(BF)
            both = dot_bt(dz[rows(c), :], wts[k, pl.ds(0, 2 * CH), :])
            back_s[k, rows(c), :] = both[:, :CH].astype(BF)

            @pl.when(t >= d)
            def _():
                back_copy(k, c, t - d).start()

            part_g[rows(c), :] = g.astype(F32) + both[:, CH:]

        for n in range(2):
            cols = pl.ds(n * CH, CH)
            first = dot_at(th[k], dz[:, cols]).astype(BF)
            right = grad[k + 1] if n == 0 else cot[...]
            second = dot_at(gated_s[k], right).astype(BF)
            for m in range(2):
                block = 2 * n + m
                lanes = slice(m * LANES, (m + 1) * LANES)
                sums[k, 0, block] = first[:HALF_ROWS, lanes]
                sums[k, 1, block, pl.ds(0, 2 * CH - HALF_ROWS), :] = first[HALF_ROWS:, lanes]
                sums[k, 1, block, pl.ds(2 * CH - HALF_ROWS, CH), :] = second[:, lanes]
        s1(k).start()

        @pl.when(i >= 1)
        def _():
            s1_to_s2(k + 1)

        @pl.when(i >= 2)
        def _():
            s2_to_s3(k + 2)

        @pl.when(i >= 3)
        def _():
            s3_to_s4(k + 3)

        return d // 2

    lax.fori_loop(0, SECTIONS, backward, jnp.int32(SPAN << (SECTIONS - 1)))

    s1_to_s2(0)
    s2_to_s3(1)
    s3_to_s4(2)
    finish_grad(0, SPAN, 0)
    s2_to_s3(0)
    s3_to_s4(1)
    finish_grad(0, SPAN, 1)
    s3_to_s4(0)

    total = z_s[x].astype(F32)
    for j in range(1, SECTIONS):
        s4_recv(j).wait_recv()
        total = total + x_r[j - 1].astype(F32)
    full[core, y, piece(z), :] = total.astype(BF)
    for j in range(1, ZS):
        s5(j, z).start()
    for j in range(1, ZS):
        s5(j, lax.rem(z - j + ZS, ZS)).wait_recv()
    for j in range(1, YS):
        s6(j, y).start()
    for j in range(1, YS):
        s6(j, lax.rem(y - j + YS, YS)).wait_recv()
    s7(core).start()
    s7(1 - core).wait_recv()
    done = pltpu.make_async_copy(full, out_sums, sem_loc.at[3])
    done.start()

    for j in range(1, SECTIONS):
        w_copy(x, j).wait_send()
        skip_copy(j).wait_send()
        skip_recv(j).wait_recv()
        for c in range(PARTS):
            ig_recv(j, c).wait_recv()
    skip_own.wait()
    for c in range(PARTS):
        ig_own(x, c).wait()
    for j in range(1, ZS):
        s5(j, z).wait_send()
    for j in range(1, YS):
        s6(j, y).wait_send()
    s7(core).wait_send()

    def drain(k, d):
        @pl.when(x != k)
        def _():
            w_mate(k, core).wait_send()
            s4(k).wait_send()
            for c in range(PARTS):
                ig_copy(k, c).wait_send()

        for c in range(PARTS):
            @pl.when(t + d < SHARDS)
            def _():
                tap_copy(k, c, t).wait_send()

            @pl.when(t >= d)
            def _():
                back_copy(k, c, t).wait_send()

        s1(k).wait_send()
        for j in range(1, YS):
            s2(k, j).wait_send()
        for j in range(1, ZS):
            s3(k, j).wait_send()
        return d * 2

    lax.fori_loop(0, SECTIONS, drain, jnp.int32(SPAN))
    done.wait()


def body(signal, skip_cot, res_cot, w_tap, w_now, w_res, w_skip):
    any_space = pl.BlockSpec(memory_space=pl.ANY)
    dma = pltpu.SemaphoreType.DMA
    n = SECTIONS
    skip_total, input_grads, sums = pl.pallas_call(
        kernel,
        out_shape=(
            jax.ShapeDtypeStruct((n, ROWS, CH), BF),
            jax.ShapeDtypeStruct((1, n, ROWS, CH), BF),
            jax.ShapeDtypeStruct((CORES, YS, HALF_ROWS, LANES), BF),
        ),
        in_specs=[any_space] * 7,
        out_specs=(any_space,) * 3,
        scratch_shapes=[
            pltpu.VMEM((n, 3 * CH, 2 * CH), BF),
            pltpu.VMEM((n + 1, ROWS, 2 * CH), BF),
            pltpu.VMEM((n, ROWS, CH), F32),
            pltpu.VMEM((n, ROWS, CH), F32),
            pltpu.VMEM((n, ROWS, CH), BF),
            pltpu.VMEM((ROWS, CH), F32),
            pltpu.VMEM((ROWS, CH), BF),
            pltpu.VMEM((ROWS, CH), BF),
            pltpu.VMEM((n + 1, ROWS, CH), BF),
            pltpu.VMEM((ROWS, 2 * CH), BF),
            pltpu.VMEM((n, ROWS, CH), BF),
            pltpu.VMEM((n, ROWS, CH), BF),
            pltpu.VMEM((ROWS, CH), F32),
            pltpu.VMEM((n, CORES, YS, HALF_ROWS, LANES), BF),
            pltpu.VMEM((n, YS, HALF_ROWS, LANES), BF),
            pltpu.VMEM((n, YS, HALF_ROWS, LANES), BF),
            pltpu.VMEM((n, YS - 1, HALF_ROWS, LANES), BF),
            pltpu.VMEM((n, HALF_ROWS, LANES), BF),
            pltpu.VMEM((n, ZS - 1, PIECE, LANES), BF),
            pltpu.VMEM((n, PIECE, LANES), BF),
            pltpu.VMEM((n - 1, PIECE, LANES), BF),
            pltpu.VMEM((CORES, YS, HALF_ROWS, LANES), BF),
            dma((7,)),
            dma((4,)),
            dma((n - 1,)), dma((n - 1,)),
            dma((n,)), dma((n,)),
            dma((n * PARTS,)), dma((n * PARTS,)),
            dma((n * PARTS,)), dma((n * PARTS,)),
            dma((n - 1,)), dma((n - 1,)),
            dma((n * PARTS,)), dma(((n - 1) * PARTS,)),
            dma((n,)), dma((n,)),
            dma((n * (YS - 1),)), dma((n * (YS - 1),)),
            dma((n * (ZS - 1),)), dma((n * (ZS - 1),)),
            dma((n,)), dma((n - 1,)),
            dma((ZS - 1,)), dma((ZS - 1,)),
            dma((YS - 1,)), dma((YS - 1,)),
            dma((1,)), dma((1,)),
        ],
        compiler_params=pltpu.CompilerParams(
            collective_id=0, has_side_effects=True, vmem_limit_bytes=56 << 20
        ),
    )(signal, skip_cot, res_cot, w_tap, w_now, w_res, w_skip)
    scale = 1.0 / math.sqrt(n * ROWS * SHARDS)
    packed = sums.astype(F32) * scale
    packed = packed.transpose(0, 2, 1, 3).reshape(1, 3 * CH, 2 * CH)
    return (
        skip_total,
        input_grads,
        packed[:, :CH],
        packed[:, CH : 2 * CH],
        packed[:, 2 * CH :, :CH],
        packed[:, 2 * CH :, CH:],
    )


def solution(mesh):
    rows3 = P(None, "tm", None)
    owned = P("section", None, None)
    return jax.shard_map(
        body,
        mesh=mesh,
        in_specs=(rows3,) * 3 + (owned,) * 4,
        out_specs=(rows3, P("section", None, "tm", None)) + (owned,) * 4,
        check_vma=False,
    )
```

time: 492 us -> 139 us (0.28)
  waiting for transfers between devices: 363 us -> 0 us
  Pallas kernels: 0 us -> 132 us
  matrix products: 35.9 us -> 0 us
  starting transfers between devices: 35.2 us -> 0 us
  blocking collectives: 25.2 us -> 0 us
  between operations: 15.1 us -> 0.68 us
  other arithmetic: 11.1 us -> 1.26 us
    psum x1 -> x0, waiting for transfers between devices: 194 us -> none  [body(): lax.psum((partial_sums[0], partial_sums[1], partial_sums[2], partial_sums...]
    pallas_call x0 -> x1, Pallas kernels: none -> 132 us  [body(): pl.pallas_call(kernel, out_shape=(jax.ShapeDtypeStruct((n, ROWS, CH), BF)...]
    reduce_scatter x4 -> x0, waiting for transfers between devices: 71.5 us -> none  [the longest x1 36.6 us: run_sequences(): lax.psum_scatter(jnp.stack([term[0] for term in term_list]), 'section', s...]
    all_gather x3 -> x0, waiting for transfers between devices: 50 us -> none  [the longest x1 26.8 us: run_sequences(): lax.all_gather(skip_running_sum.astype(jnp.bfloat16), 'section', axis=0,...]
    ppermute x8 -> x0, waiting for transfers between devices: 46.2 us -> none  [passed_along(): return lax.ppermute(x, axis, pairs)]
    dot_general x47 -> x0, matrix products: 35.9 us -> none  [the longest x31 25.9 us: flat_dot(): jnp.dot(left.reshape(-1, left.shape[-1]), right, preferred_element_type=j...]
    ppermute x8 -> x0, starting transfers between devices: 31.2 us -> none  [passed_along(): return lax.ppermute(x, axis, pairs)]
    all_gather x2 -> x0, blocking collectives: 25.2 us -> none  [the longest x1 13.3 us: run_sequences(): lax.all_gather(w_skip, 'section', axis=0, tiled=True)]
  transfers between devices with their start and end apart: 17 -> 0, of which waited for: 12 -> 0; matrix products, arithmetic and copies ran while one was open for 7% -> 0% of each run, Pallas kernels for 0% -> 0%
where the time goes in v1:
time: 139 us
  Pallas kernels  132 us (95%)
  local copies, waits for them, and re-layouts  5.45 us (4%)
    pallas_call x1, Pallas kernels, body(): pl.pallas_call(kernel, out_shape=(jax.ShapeDtypeStruct((n, ROWS, CH), BF)...  132 us

profile of v1, /device:TPU:1, one launch (start us, length us, event | category | flops | bytes accessed | tf_op | source)
XLA Modules:
  0.0 138.9 jit_solution(15629867548362016103)
XLA Ops:
  0.6 131.5 %shard_map.118 = (bf16[4,512,256]{2,1,0:T(8,128)(2,1)}, bf16[1,4,512,256]{3,2,1,0:T(8,128)(2,1)}, bf16[2,4,384,128]{3,2,1,0:T(8,128)(2,1)}) custom-call(bf16[4,512,256]{2,1,0:T(8,128)(2,1)} %signal.1, bf16[4,512,256]{2,1,0:T(8,128)(2,1)} %skip_cot.1, bf16[4,512,256]{2,1,0:T(8,128)(2,1)} %res_cot.1, bf16[1,256,512]{2,1,0:T(8,128)(2,1)} %w_tap.1, ...), custom_call_target="tpu_custom_call" | custom-call | tf_op jit(solution)/shard_map/pallas_call | solution.py:454
  132.2 1.3 multiply_bitcast_fusion
  133.5 1.0 copy.13
  134.5 0.6 reshape.15
  135.1 0.0 copy-start.1
  135.1 1.0 fusion.1
  136.2 0.0 copy-start
  136.2 0.8 fusion
  137.0 0.0 copy-done.1
  137.0 1.0 copy.16
  138.0 0.0 copy-done
  138.0 1.0 copy.17
Async XLA Ops:
  135.1 1.9 %copy-start.1 = (bf16[4,512,256]{2,1,0:T(8,128)(2,1)S(1)}, bf16[4,512,256]{2,1,0:T(8,128)(2,1)}, u32[]{:S(2)}) copy-start(bf16[4,512,256]{2,1,0:T(8,128)(2,1)} %get-tuple-element.22) | copy-start | bytes 3145732
  136.2 1.8 %copy-start = (bf16[1,4,512,256]{3,2,1,0:T(8,128)(2,1)S(1)}, bf16[1,4,512,256]{3,2,1,0:T(8,128)(2,1)}, u32[]{:S(2)}) copy-start(bf16[1,4,512,256]{3,2,1,0:T(8,128)(2,1)} %get-tuple-element.23) | copy-start | bytes 3145732

commit v2 on v1

v2 whole, which is shorter than its diff:
```python
import math

import jax
import jax.numpy as jnp
from jax import lax
from jax.experimental import pallas as pl
from jax.experimental.pallas import tpu as pltpu
from jax.sharding import PartitionSpec as P

MESH = pl.DeviceIdType.MESH
BF = jnp.bfloat16
F32 = jnp.float32

SECTIONS = 4
YS, ZS, CORES = 4, 8, 2
SHARDS = YS * ZS * CORES
ROWS, CH = 512, 256
GROUP = 16
BLOCK = ROWS // GROUP
LEAD = ROWS // 2
PARTS = 2
PART = ROWS // PARTS
HALF_ROWS = 384
PIECE = HALF_ROWS // ZS
LANES = 128


def dot(a, b):
    return jnp.dot(a, b, preferred_element_type=F32)


def dot_bt(a, b):
    return lax.dot_general(a, b, (((1,), (1,)), ((), ())), preferred_element_type=F32)


def dot_at(a, b):
    return lax.dot_general(a, b, (((0,), (0,)), ((), ())), preferred_element_type=F32)


def kernel(
    signal, skip_cot, res_cot, w_tap, w_now, w_res, w_skip,
    out_skip, out_grads, out_tap, out_now, out_res, out_wskip,
    wts, hp, act, sig, gated_s, skip_acc, skip_out, skip_t, cot, grad, dz, bp, part_g,
    sums, pair_r, pair_s, y_r, y_s, z_r, z_s, x_r, full,
    sem_in, sem_loc, w_ss, w_rs, wp_ss, wp_rs, in_ss, in_rs,
    skt_ss, skt_rs, skip_ss, skip_rs, ig_ss, ig_rs, s1_ss, s1_rs, s2_ss, s2_rs, s3_ss, s3_rs,
    s4_ss, s4_rs, s5_ss, s5_rs, s6_ss, s6_rs, s7_ss, s7_rs,
):
    x = lax.axis_index("section")
    t = lax.axis_index("tm")
    core = lax.rem(t, CORES)
    z = lax.rem(t // CORES, ZS)
    y = t // (CORES * ZS)
    z_half, z_odd = z // 2, lax.rem(z, 2)
    me = y * 4 + z_half
    mate = t + 1 - 2 * core

    def at_x(j):
        return lax.rem(x + j + SECTIONS, SECTIONS)

    def at_y(j):
        return (lax.rem(y + j + YS, YS) * ZS + z) * CORES + core

    def at_z(j):
        return (y * ZS + lax.rem(z + j + ZS, ZS)) * CORES + core

    def member(j):
        dy, dz = j // 4, j % 4
        py, pz = lax.rem(y + dy, YS), lax.rem(z_half + dz, 4)
        return py * 4 + pz, (py * ZS + pz * 2 + z_odd) * CORES + core

    def rows(c):
        return pl.ds(c * PART, PART)

    def block(i, lead=0):
        return pl.ds(pl.multiple_of(lead + i * BLOCK, BLOCK), BLOCK)

    def remote(src, dst, ss, rs, to_x, to_t):
        return pltpu.make_async_remote_copy(
            src_ref=src, dst_ref=dst, send_sem=ss, recv_sem=rs,
            device_id=(to_x, to_t), device_id_type=MESH,
        )

    def w_copy(layer, j):
        half = pl.ds(core * HALF_ROWS, HALF_ROWS)
        return remote(
            wts.at[layer, half], wts.at[layer, half],
            w_ss.at[j - 1], w_rs.at[j - 1], at_x(j), t,
        )

    def w_recv(layer):
        j = lax.rem(x - layer + SECTIONS, SECTIONS)
        half = pl.ds(core * HALF_ROWS, HALF_ROWS)
        return remote(
            wts.at[layer, half], wts.at[layer, half],
            w_ss.at[j - 1], w_rs.at[j - 1], layer, t,
        )

    def w_mate(layer, whose):
        half = pl.ds(whose * HALF_ROWS, HALF_ROWS)
        return remote(
            wts.at[layer, half], wts.at[layer, half],
            wp_ss.at[layer], wp_rs.at[layer], x, mate,
        )

    inputs = (signal, skip_cot, res_cot)
    places = ((hp.at[0], LEAD), (cot, 0), (grad.at[SECTIONS], 0))

    def spread(n, j):
        place, shard = member(j)
        to, lead = places[n]
        return remote(
            inputs[n].at[x, block(place)], to.at[block(me, lead)],
            in_ss.at[n], in_rs.at[n], x, shard,
        )

    def spread_own(n):
        to, lead = places[n]
        return pltpu.make_async_copy(
            inputs[n].at[x, block(me)], to.at[block(me, lead)], sem_in.at[4 + n]
        )

    def others(ss, rs):
        some = cot.at[pl.ds(0, ROWS - BLOCK)]
        return remote(some, some, ss, rs, x, mate)

    def whole(ss, rs):
        return remote(cot, cot, ss, rs, x, mate)

    def skip_back(j):
        place, shard = member(j)
        return remote(
            skip_out.at[block(place)], skip_t.at[block(me)], skt_ss.at[0], skt_rs.at[0], x, shard
        )

    def skip_copy(j):
        return remote(
            skip_t, out_skip.at[x], skip_ss.at[j - 1], skip_rs.at[j - 1], at_x(j), t
        )

    def skip_recv(j):
        return remote(
            skip_t, out_skip.at[at_x(-j)], skip_ss.at[j - 1], skip_rs.at[j - 1], at_x(-j), t
        )

    def ig_copy(layer, j):
        place, shard = member(j)
        return remote(
            grad.at[layer, block(place)], out_grads.at[0, x, block(me)],
            ig_ss.at[layer], ig_rs.at[lax.rem(layer - x + SECTIONS, SECTIONS)], layer, shard,
        )

    def ig_own(layer):
        return pltpu.make_async_copy(
            grad.at[layer, block(me)], out_grads.at[0, x, block(me)], sem_loc.at[0]
        )

    def s1(layer):
        return remote(
            sums.at[layer, 1 - core], pair_r.at[layer],
            s1_ss.at[layer], s1_rs.at[layer], x, mate,
        )

    def s2(layer, j):
        return remote(
            pair_s.at[layer, lax.rem(y + j, YS)], y_r.at[layer, j - 1],
            s2_ss.at[layer * 3 + j - 1], s2_rs.at[layer * 3 + j - 1], x, at_y(j),
        )

    def piece(i):
        return pl.ds(pl.multiple_of(i * PIECE, 16), PIECE)

    def s3(layer, j):
        return remote(
            y_s.at[layer, piece(lax.rem(z + j, ZS))], z_r.at[layer, j - 1],
            s3_ss.at[layer * 7 + j - 1], s3_rs.at[layer * 7 + j - 1], x, at_z(j),
        )

    def s4(layer):
        j = lax.rem(layer - x + SECTIONS, SECTIONS)
        return remote(
            z_s.at[layer], x_r.at[j - 1], s4_ss.at[layer], s4_rs.at[j - 1], layer, t
        )

    def s4_recv(j):
        return remote(z_s.at[0], x_r.at[j - 1], s4_ss.at[0], s4_rs.at[j - 1], at_x(-j), t)

    def s5(j, whose):
        return remote(
            full.at[core, y, piece(whose)], full.at[core, y, piece(whose)],
            s5_ss.at[j - 1], s5_rs.at[j - 1], x, at_z(j),
        )

    def s6(j, whose):
        return remote(
            full.at[core, whose], full.at[core, whose],
            s6_ss.at[j - 1], s6_rs.at[j - 1], x, at_y(j),
        )

    def s7(whose):
        return remote(full.at[whose], full.at[whose], s7_ss.at[0], s7_rs.at[0], x, mate)

    loads = [
        pltpu.make_async_copy(w_tap.at[0], wts.at[x, pl.ds(0, CH)], sem_in.at[0]),
        pltpu.make_async_copy(w_now.at[0], wts.at[x, pl.ds(CH, CH)], sem_in.at[1]),
        pltpu.make_async_copy(
            w_res.at[0], wts.at[x, pl.ds(2 * CH, CH), pl.ds(0, CH)], sem_in.at[2]
        ),
        pltpu.make_async_copy(
            w_skip.at[0], wts.at[x, pl.ds(2 * CH, CH), pl.ds(CH, CH)], sem_in.at[3]
        ),
    ] + [spread_own(n) for n in range(3)]
    for load in loads:
        load.start()

    barrier = pltpu.get_barrier_semaphore()
    peers = [(x, mate)] + [(x, at_z(j)) for j in (1, 3, 5, 7)]
    peers += [(x, member(j)[1]) for j in range(1, GROUP)]
    peers += [(at_x(i), member(j)[1]) for i in range(1, SECTIONS) for j in range(GROUP)]
    for peer in peers:
        pl.semaphore_signal(barrier, inc=1, device_id=peer, device_id_type=MESH)

    for layer in range(SECTIONS):
        hp[layer, pl.ds(0, LEAD), :] = jnp.zeros((LEAD, CH), BF)
    bp[pl.ds(ROWS, LEAD), :] = jnp.zeros((LEAD, CH), BF)
    skip_acc[...] = jnp.zeros((ROWS, CH), F32)
    pl.semaphore_wait(barrier, len(peers))

    for j in range(1, GROUP):
        spread(0, j).start()
    for load in loads[:4]:
        load.wait()
    for j in range(1, SECTIONS):
        w_copy(x, j).start()
    for n in (1, 2):
        for j in range(1, GROUP):
            spread(n, j).start()

    def w_forward(layer):
        @pl.when(x != layer)
        def _():
            w_recv(layer).wait_recv()
            w_mate(layer, core).start()

    for layer in range(SECTIONS):
        w_forward(layer)
    loads[4].wait()
    others(in_ss.at[0], in_rs.at[0]).wait_recv()

    def tap_rows(c, shift):
        return pl.ds(pl.multiple_of(LEAD + c * PART - shift, BLOCK), PART)

    def forward(k, shift):
        @pl.when(x != k)
        def _():
            w_mate(k, 1 - core).wait_recv()

        for c in range(PARTS):
            here = pl.ds(LEAD + c * PART, PART)
            h = hp[k, here, :]
            pre = dot(hp[k, tap_rows(c, shift), :], wts[k, pl.ds(0, CH), :]) + dot(
                h, wts[k, pl.ds(CH, CH), :]
            )
            a = jnp.tanh(pre[:, :CH])
            s = jax.nn.sigmoid(pre[:, CH:])
            act[k, rows(c), :] = a
            sig[k, rows(c), :] = s
            gated = (a * s).astype(BF)
            gated_s[k, rows(c), :] = gated
            out = dot(gated, wts[k, pl.ds(2 * CH, CH), :])
            skip_acc[rows(c), :] += out[:, CH:]
            hp[k + 1, here, :] = (h.astype(F32) + out[:, :CH]).astype(BF)

        return shift * 2

    lax.fori_loop(0, SECTIONS, forward, jnp.int32(BLOCK))

    skip_out[...] = skip_acc[...].astype(BF)
    for j in range(1, GROUP):
        skip_back(j).start()
    skip_mine = pltpu.make_async_copy(
        skip_out.at[block(me)], skip_t.at[block(me)], sem_loc.at[1]
    )
    skip_mine.start()

    def s1_to_s2(layer):
        s1(layer).wait_recv()
        pair_s[layer] = (
            sums[layer, core].astype(F32) + pair_r[layer].astype(F32)
        ).astype(BF)
        for j in range(1, YS):
            s2(layer, j).start()

    def s2_to_s3(layer):
        total = pair_s[layer, y].astype(F32)
        for j in range(1, YS):
            s2(layer, j).wait_recv()
            total = total + y_r[layer, j - 1].astype(F32)
        y_s[layer] = total.astype(BF)
        for j in range(1, ZS):
            s3(layer, j).start()

    def s3_to_s4(layer):
        total = y_s[layer, piece(z), :].astype(F32)
        for j in range(1, ZS):
            s3(layer, j).wait_recv()
            total = total + z_r[layer, j - 1].astype(F32)
        z_s[layer] = total.astype(BF)

        @pl.when(x != layer)
        def _():
            s4(layer).start()

    for n in (1, 2):
        loads[4 + n].wait()
        others(in_ss.at[n], in_rs.at[n]).wait_recv()

    def backward(i, shift):
        k = SECTIONS - 1 - i
        for c in range(PARTS):
            g = grad[k + 1, rows(c), :]
            du = dot_bt(g, wts[k, pl.ds(2 * CH, CH), pl.ds(0, CH)]) + dot_bt(
                cot[rows(c), :], wts[k, pl.ds(2 * CH, CH), pl.ds(CH, CH)]
            )
            a = act[k, rows(c), :]
            s = sig[k, rows(c), :]
            us = du * s
            dz[rows(c), pl.ds(0, CH)] = (us * (1.0 - a * a)).astype(BF)
            dz[rows(c), pl.ds(CH, CH)] = (us * a * (1.0 - s)).astype(BF)
            both = dot_bt(dz[rows(c), :], wts[k, pl.ds(0, 2 * CH), :])
            bp[rows(c), :] = both[:, :CH].astype(BF)
            part_g[rows(c), :] = g.astype(F32) + both[:, CH:]

        for c in range(PARTS):
            later = pl.ds(pl.multiple_of(c * PART + shift, BLOCK), PART)
            grad[k, rows(c), :] = (part_g[rows(c), :] + bp[later, :].astype(F32)).astype(BF)

        for n in range(2):
            cols = pl.ds(n * CH, CH)
            right = dz[:, cols]
            tap = hp[k, pl.ds(pl.multiple_of(LEAD - shift, BLOCK), ROWS), :]
            tap_sum = dot_at(tap, right).astype(BF)
            now_sum = dot_at(hp[k, pl.ds(LEAD, ROWS), :], right).astype(BF)
            out_sum = dot_at(gated_s[k], grad[k + 1] if n == 0 else cot[...]).astype(BF)
            rest = HALF_ROWS - CH
            for m in range(2):
                at = 2 * n + m
                lanes = slice(m * LANES, (m + 1) * LANES)
                sums[k, 0, at, pl.ds(0, CH), :] = tap_sum[:, lanes]
                sums[k, 0, at, pl.ds(CH, rest), :] = now_sum[:rest, lanes]
                sums[k, 1, at, pl.ds(0, CH - rest), :] = now_sum[rest:, lanes]
                sums[k, 1, at, pl.ds(CH - rest, CH), :] = out_sum[:, lanes]
        s1(k).start()

        @pl.when(x != k)
        def _():
            ig_copy(k, 0).start()

        @pl.when(x == k)
        def _():
            ig_own(k).start()

        for j in range(1, GROUP):
            ig_copy(k, j).start()

        @pl.when(i >= 1)
        def _():
            s1_to_s2(k + 1)

        return shift // 2

    lax.fori_loop(0, SECTIONS, backward, jnp.int32(BLOCK << (SECTIONS - 1)))

    s1_to_s2(0)
    skip_mine.wait()
    others(skt_ss.at[0], skt_rs.at[0]).wait_recv()
    for j in range(1, SECTIONS):
        skip_copy(j).start()
    skip_own = pltpu.make_async_copy(skip_t, out_skip.at[x], sem_loc.at[2])
    skip_own.start()
    s2_to_s3(3)
    s2_to_s3(2)
    s3_to_s4(3)
    s2_to_s3(1)
    s3_to_s4(2)
    s2_to_s3(0)
    s3_to_s4(1)
    s3_to_s4(0)

    total = z_s[x].astype(F32)
    for j in range(1, SECTIONS):
        s4_recv(j).wait_recv()
        total = total + x_r[j - 1].astype(F32)
    full[core, y, piece(z), :] = total.astype(BF)
    for j in range(1, ZS):
        s5(j, z).start()
    for j in range(1, ZS):
        s5(j, lax.rem(z - j + ZS, ZS)).wait_recv()
    for j in range(1, YS):
        s6(j, y).start()
    for j in range(1, YS):
        s6(j, lax.rem(y - j + YS, YS)).wait_recv()
    s7(core).start()
    s7(1 - core).wait_recv()
    scale = 1.0 / math.sqrt(SECTIONS * ROWS * SHARDS)
    rest = HALF_ROWS - CH
    for at in range(YS):
        lanes = pl.ds(at * LANES, LANES)
        out_tap[0, :, lanes] = full[0, at, pl.ds(0, CH), :].astype(F32) * scale
        out_now[0, pl.ds(0, rest), lanes] = full[0, at, pl.ds(CH, rest), :].astype(F32) * scale
        out_now[0, pl.ds(rest, CH - rest), lanes] = (
            full[1, at, pl.ds(0, CH - rest), :].astype(F32) * scale
        )
        out = out_res if at < 2 else out_wskip
        lanes = pl.ds(at % 2 * LANES, LANES)
        out[0, :, lanes] = full[1, at, pl.ds(CH - rest, CH), :].astype(F32) * scale

    for n in range(3):
        others(in_ss.at[n], in_rs.at[n]).wait_send()
    others(skt_ss.at[0], skt_rs.at[0]).wait_send()
    others(ig_ss.at[x], ig_rs.at[0]).wait_recv()
    others(ig_ss.at[x], ig_rs.at[0]).wait_send()
    for j in range(1, SECTIONS):
        w_copy(x, j).wait_send()
        skip_copy(j).wait_send()
        skip_recv(j).wait_recv()
        whole(ig_ss.at[0], ig_rs.at[j]).wait_recv()
    skip_own.wait()
    ig_own(x).wait()
    for j in range(1, ZS):
        s5(j, z).wait_send()
    for j in range(1, YS):
        s6(j, y).wait_send()
    s7(core).wait_send()

    def drain(k, carry):
        @pl.when(x != k)
        def _():
            w_mate(k, core).wait_send()
            s4(k).wait_send()
            whole(ig_ss.at[k], ig_rs.at[0]).wait_send()

        s1(k).wait_send()
        for j in range(1, YS):
            s2(k, j).wait_send()
        for j in range(1, ZS):
            s3(k, j).wait_send()
        return carry

    lax.fori_loop(0, SECTIONS, drain, jnp.int32(0))


def body(signal, skip_cot, res_cot, w_tap, w_now, w_res, w_skip):
    any_space = pl.BlockSpec(memory_space=pl.ANY)
    vmem = pl.BlockSpec(memory_space=pltpu.VMEM)
    dma = pltpu.SemaphoreType.DMA
    n = SECTIONS
    return pl.pallas_call(
        kernel,
        out_shape=(
            jax.ShapeDtypeStruct((n, ROWS, CH), BF),
            jax.ShapeDtypeStruct((1, n, ROWS, CH), BF),
            jax.ShapeDtypeStruct((1, CH, 2 * CH), F32),
            jax.ShapeDtypeStruct((1, CH, 2 * CH), F32),
            jax.ShapeDtypeStruct((1, CH, CH), F32),
            jax.ShapeDtypeStruct((1, CH, CH), F32),
        ),
        in_specs=[any_space] * 7,
        out_specs=(any_space,) * 2 + (vmem,) * 4,
        scratch_shapes=[
            pltpu.VMEM((n, 3 * CH, 2 * CH), BF),
            pltpu.VMEM((n + 1, LEAD + ROWS, CH), BF),
            pltpu.VMEM((n, ROWS, CH), F32),
            pltpu.VMEM((n, ROWS, CH), F32),
            pltpu.VMEM((n, ROWS, CH), BF),
            pltpu.VMEM((ROWS, CH), F32),
            pltpu.VMEM((ROWS, CH), BF),
            pltpu.VMEM((ROWS, CH), BF),
            pltpu.VMEM((ROWS, CH), BF),
            pltpu.VMEM((n + 1, ROWS, CH), BF),
            pltpu.VMEM((ROWS, 2 * CH), BF),
            pltpu.VMEM((ROWS + LEAD, CH), BF),
            pltpu.VMEM((ROWS, CH), F32),
            pltpu.VMEM((n, CORES, YS, HALF_ROWS, LANES), BF),
            pltpu.VMEM((n, YS, HALF_ROWS, LANES), BF),
            pltpu.VMEM((n, YS, HALF_ROWS, LANES), BF),
            pltpu.VMEM((n, YS - 1, HALF_ROWS, LANES), BF),
            pltpu.VMEM((n, HALF_ROWS, LANES), BF),
            pltpu.VMEM((n, ZS - 1, PIECE, LANES), BF),
            pltpu.VMEM((n, PIECE, LANES), BF),
            pltpu.VMEM((n - 1, PIECE, LANES), BF),
            pltpu.VMEM((CORES, YS, HALF_ROWS, LANES), BF),
            dma((7,)),
            dma((3,)),
            dma((n - 1,)), dma((n - 1,)),
            dma((n,)), dma((n,)),
            dma((3,)), dma((3,)),
            dma((1,)), dma((1,)),
            dma((n - 1,)), dma((n - 1,)),
            dma((n,)), dma((n,)),
            dma((n,)), dma((n,)),
            dma((n * (YS - 1),)), dma((n * (YS - 1),)),
            dma((n * (ZS - 1),)), dma((n * (ZS - 1),)),
            dma((n,)), dma((n - 1,)),
            dma((ZS - 1,)), dma((ZS - 1,)),
            dma((YS - 1,)), dma((YS - 1,)),
            dma((1,)), dma((1,)),
        ],
        compiler_params=pltpu.CompilerParams(
            collective_id=0, has_side_effects=True, vmem_limit_bytes=56 << 20
        ),
    )(signal, skip_cot, res_cot, w_tap, w_now, w_res, w_skip)


def solution(mesh):
    rows3 = P(None, "tm", None)
    owned = P("section", None, None)
    return jax.shard_map(
        body,
        mesh=mesh,
        in_specs=(rows3,) * 3 + (owned,) * 4,
        out_specs=(rows3, P("section", None, "tm", None)) + (owned,) * 4,
        check_vma=False,
    )
```

time: 139 us -> 105 us (0.76)
  Pallas kernels: 132 us -> 96.3 us
  local copies, waits for them, and re-layouts: 5.45 us -> 7.82 us
    pallas_call x1, Pallas kernels: 132 us -> 96.3 us  [body(): pl.pallas_call(kernel, out_shape=(jax.ShapeDtypeStruct((n, ROWS, CH), BF)...]
    unnamed x6 -> x16, local copies, waits for them, and re-layouts: 1.95 us -> 7.82 us
    slice x2 -> x0, local copies, waits for them, and re-layouts: 1.86 us -> none  [the longest x1 1.03 us: body(): packed[:, CH:2 * CH]]
where the time goes in v2:
time: 105 us
  Pallas kernels  96.3 us (92%)
  local copies, waits for them, and re-layouts  7.82 us (7%)
    pallas_call x1, Pallas kernels, body(): pl.pallas_call(kernel, out_shape=(jax.ShapeDtypeStruct((n, ROWS, CH), BF)...  96.3 us
    unnamed x16, local copies, waits for them, and re-layouts  7.82 us

profile of v2, /device:TPU:1, one launch (start us, length us, event | category | flops | bytes accessed | tf_op | source)
XLA Modules:
  0.0 104.8 jit_solution(3930554893800924316)
XLA Ops:
  0.6 96.3 %shard_map.118 = (bf16[4,512,256]{2,1,0:T(8,128)(2,1)}, bf16[1,4,512,256]{3,2,1,0:T(8,128)(2,1)}, f32[1,256,512]{2,1,0:T(8,128)}, f32[1,256,512]{2,1,0:T(8,128)}...) custom-call(bf16[4,512,256]{2,1,0:T(8,128)(2,1)} %signal.1, bf16[4,512,256]{2,1,0:T(8,128)(2,1)} %skip_cot.1, ...), custom_call_target="tpu_custom_call" | custom-call | tf_op jit(solution)/shard_map/pallas_call | solution.py:458
  96.9 0.0 copy-start
  97.0 2.4 %copy.19 = bf16[4,512,256]{2,1,0:T(8,128)(2,1)} copy(bf16[4,512,256]{2,1,0:T(8,128)(2,1)} %get-tuple-element.12) | data formatting | bytes 2097152
  99.3 0.0 copy-done
  99.3 0.0 copy-start.2
  99.3 1.0 copy.20
  100.3 0.4 copy-done.2
  100.7 0.0 copy-start.1
  100.7 0.8 copy.21
  101.5 0.4 copy-done.1
  101.9 0.0 copy-start.4
  101.9 0.8 copy.22
  102.7 0.3 copy-done.4
  103.0 0.0 copy-start.3
  103.0 0.7 copy.23
  103.7 0.3 copy-done.3
  104.1 0.7 copy.24
Async XLA Ops:
  96.9 2.4 %copy-start = (bf16[1,4,512,256]{3,2,1,0:T(8,128)(2,1)S(1)}, bf16[1,4,512,256]{3,2,1,0:T(8,128)(2,1)}, u32[]{:S(2)}) copy-start(bf16[1,4,512,256]{3,2,1,0:T(8,128)(2,1)} %get-tuple-element.13) | copy-start | bytes 3145732
  99.3 1.4 %copy-start.2 = (f32[1,256,512]{2,1,0:T(8,128)S(1)}, f32[1,256,512]{2,1,0:T(8,128)}, u32[]{:S(2)}) copy-start(f32[1,256,512]{2,1,0:T(8,128)} %get-tuple-element.14) | copy-start | bytes 1572868
  100.7 1.2 %copy-start.1 = (f32[1,256,512]{2,1,0:T(8,128)S(1)}, f32[1,256,512]{2,1,0:T(8,128)}, u32[]{:S(2)}) copy-start(f32[1,256,512]{2,1,0:T(8,128)} %get-tuple-element.15) | copy-start | bytes 1572868
  101.9 1.1 %copy-start.4 = (f32[1,256,256]{2,1,0:T(8,128)S(1)}, f32[1,256,256]{2,1,0:T(8,128)}, u32[]{:S(2)}) copy-start(f32[1,256,256]{2,1,0:T(8,128)} %get-tuple-element.16) | copy-start | bytes 786436
  103.0 1.0 copy-start.3

commit v3 on v2

--- a/solution.py
+++ b/solution.py
@@ -39,12 +39,12 @@
 
 def kernel(
     signal, skip_cot, res_cot, w_tap, w_now, w_res, w_skip,
-    out_skip, out_grads, out_tap, out_now, out_res, out_wskip,
+    out_skip, out_grads, out_sums,
     wts, hp, act, sig, gated_s, skip_acc, skip_out, skip_t, cot, grad, dz, bp, part_g,
-    sums, pair_r, pair_s, y_r, y_s, z_r, z_s, x_r, full,
+    sums, pair_r, pair_s, y_r, y_s, x_r, x_s, z_r, full,
     sem_in, sem_loc, w_ss, w_rs, wp_ss, wp_rs, in_ss, in_rs,
     skt_ss, skt_rs, skip_ss, skip_rs, ig_ss, ig_rs, s1_ss, s1_rs, s2_ss, s2_rs, s3_ss, s3_rs,
-    s4_ss, s4_rs, s5_ss, s5_rs, s6_ss, s6_rs, s7_ss, s7_rs,
+    s4_ss, s4_rs, s5_ss, s5_rs, s6_ss, s6_rs, s7_ss, s7_rs, ready,
 ):
     x = lax.axis_index("section")
     t = lax.axis_index("tm")
@@ -81,20 +81,18 @@
             device_id=(to_x, to_t), device_id_type=MESH,
         )
 
-    def w_copy(layer, j):
-        half = pl.ds(core * HALF_ROWS, HALF_ROWS)
-        return remote(
-            wts.at[layer, half], wts.at[layer, half],
-            w_ss.at[j - 1], w_rs.at[j - 1], at_x(j), t,
-        )
-
-    def w_recv(layer):
-        j = lax.rem(x - layer + SECTIONS, SECTIONS)
-        half = pl.ds(core * HALF_ROWS, HALF_ROWS)
-        return remote(
-            wts.at[layer, half], wts.at[layer, half],
-            w_ss.at[j - 1], w_rs.at[j - 1], layer, t,
-        )
+    def w_copy(layer, part, way, n):
+        start = core * HALF_ROWS + part * (HALF_ROWS // 2)
+        here = wts.at[layer, pl.ds(pl.multiple_of(start, 64), HALF_ROWS // 2)]
+        return remote(here, here, w_ss.at[n], w_rs.at[layer * 2 + part], at_x(way), t)
+
+    def w_sends():
+        return [w_copy(x, 0, 1, 0), w_copy(x, 1, -1, 1), w_copy(x, 1, 1, 2), w_copy(x, 0, -1, 3)] + [
+            w_copy(at_x(-1), 0, 1, 4), w_copy(at_x(1), 1, -1, 5)
+        ]
+
+    def w_recv(layer, part):
+        w_copy(layer, part, 1, 0).wait_recv()
 
     def w_mate(layer, whose):
         half = pl.ds(whose * HALF_ROWS, HALF_ROWS)
@@ -170,20 +168,20 @@
     def piece(i):
         return pl.ds(pl.multiple_of(i * PIECE, 16), PIECE)
 
-    def s3(layer, j):
-        return remote(
-            y_s.at[layer, piece(lax.rem(z + j, ZS))], z_r.at[layer, j - 1],
-            s3_ss.at[layer * 7 + j - 1], s3_rs.at[layer * 7 + j - 1], x, at_z(j),
-        )
-
-    def s4(layer):
+    def s3(layer):
         j = lax.rem(layer - x + SECTIONS, SECTIONS)
         return remote(
-            z_s.at[layer], x_r.at[j - 1], s4_ss.at[layer], s4_rs.at[j - 1], layer, t
-        )
-
-    def s4_recv(j):
-        return remote(z_s.at[0], x_r.at[j - 1], s4_ss.at[0], s4_rs.at[j - 1], at_x(-j), t)
+            y_s.at[layer], x_r.at[j - 1], s3_ss.at[layer], s3_rs.at[j - 1], layer, t
+        )
+
+    def s3_recv(j):
+        return remote(y_s.at[0], x_r.at[j - 1], s3_ss.at[0], s3_rs.at[j - 1], at_x(-j), t)
+
+    def s4(j):
+        return remote(
+            x_s.at[piece(lax.rem(z + j, ZS))], z_r.at[j - 1],
+            s4_ss.at[j - 1], s4_rs.at[j - 1], x, at_z(j),
+        )
 
     def s5(j, whose):
         return remote(
@@ -191,13 +189,16 @@
             s5_ss.at[j - 1], s5_rs.at[j - 1], x, at_z(j),
         )
 
-    def s6(j, whose):
-        return remote(
-            full.at[core, whose], full.at[core, whose],
-            s6_ss.at[j - 1], s6_rs.at[j - 1], x, at_y(j),
-        )
-
-    def s7(whose):
+    def s6(j, whose, part):
+        here = full.at[core, whose, piece(part)]
+        n = (j - 1) * ZS + part
+        return remote(here, here, s6_ss.at[n], s6_rs.at[n], x, at_y(j))
+
+    def s7(whose, part):
+        here = full.at[core, whose, piece(part)]
+        return remote(here, here, s7_ss.at[0], s7_rs.at[0], x, mate)
+
+    def s7_all(whose):
         return remote(full.at[whose], full.at[whose], s7_ss.at[0], s7_rs.at[0], x, mate)
 
     loads = [
@@ -216,7 +217,7 @@
     barrier = pltpu.get_barrier_semaphore()
     peers = [(x, mate)] + [(x, at_z(j)) for j in (1, 3, 5, 7)]
     peers += [(x, member(j)[1]) for j in range(1, GROUP)]
-    peers += [(at_x(i), member(j)[1]) for i in range(1, SECTIONS) for j in range(GROUP)]
+    peers += [(at_x(j), t) for j in range(1, SECTIONS)]
     for peer in peers:
         pl.semaphore_signal(barrier, inc=1, device_id=peer, device_id_type=MESH)
 
@@ -225,25 +226,32 @@
     bp[pl.ds(ROWS, LEAD), :] = jnp.zeros((LEAD, CH), BF)
     skip_acc[...] = jnp.zeros((ROWS, CH), F32)
     pl.semaphore_wait(barrier, len(peers))
+    for j in range(1, SECTIONS):
+        pl.semaphore_signal(ready, inc=1, device_id=(at_x(j), t), device_id_type=MESH)
 
     for j in range(1, GROUP):
         spread(0, j).start()
     for load in loads[:4]:
         load.wait()
-    for j in range(1, SECTIONS):
-        w_copy(x, j).start()
+    weights = w_sends()
+    for copy in weights[:4]:
+        copy.start()
     for n in (1, 2):
         for j in range(1, GROUP):
             spread(n, j).start()
 
-    def w_forward(layer):
-        @pl.when(x != layer)
-        def _():
-            w_recv(layer).wait_recv()
-            w_mate(layer, core).start()
-
-    for layer in range(SECTIONS):
-        w_forward(layer)
+    left, right, across = at_x(-1), at_x(1), at_x(2)
+    w_recv(left, 0)
+    weights[4].start()
+    w_recv(right, 1)
+    weights[5].start()
+    w_recv(left, 1)
+    w_mate(left, core).start()
+    w_recv(right, 0)
+    w_mate(right, core).start()
+    w_recv(across, 0)
+    w_recv(across, 1)
+    w_mate(across, core).start()
     loads[4].wait()
     others(in_ss.at[0], in_rs.at[0]).wait_recv()
 
@@ -276,12 +284,6 @@
     lax.fori_loop(0, SECTIONS, forward, jnp.int32(BLOCK))
 
     skip_out[...] = skip_acc[...].astype(BF)
-    for j in range(1, GROUP):
-        skip_back(j).start()
-    skip_mine = pltpu.make_async_copy(
-        skip_out.at[block(me)], skip_t.at[block(me)], sem_loc.at[1]
-    )
-    skip_mine.start()
 
     def s1_to_s2(layer):
         s1(layer).wait_recv()
@@ -297,23 +299,33 @@
             s2(layer, j).wait_recv()
             total = total + y_r[layer, j - 1].astype(F32)
         y_s[layer] = total.astype(BF)
-        for j in range(1, ZS):
-            s3(layer, j).start()
-
-    def s3_to_s4(layer):
-        total = y_s[layer, piece(z), :].astype(F32)
-        for j in range(1, ZS):
-            s3(layer, j).wait_recv()
-            total = total + z_r[layer, j - 1].astype(F32)
-        z_s[layer] = total.astype(BF)
 
         @pl.when(x != layer)
         def _():
-            s4(layer).start()
+            s3(layer).start()
+
+    def ig_send(layer):
+        @pl.when(x != layer)
+        def _():
+            ig_copy(layer, 0).start()
+
+        @pl.when(x == layer)
+        def _():
+            ig_own(layer).start()
+
+        for j in range(1, GROUP):
+            ig_copy(layer, j).start()
 
     for n in (1, 2):
         loads[4 + n].wait()
         others(in_ss.at[n], in_rs.at[n]).wait_recv()
+    for j in range(1, GROUP):
+        skip_back(j).start()
+    skip_mine = pltpu.make_async_copy(
+        skip_out.at[block(me)], skip_t.at[block(me)], sem_loc.at[1]
+    )
+    skip_mine.start()
+    pl.semaphore_wait(ready, SECTIONS - 1)
 
     def backward(i, shift):
         k = SECTIONS - 1 - i
@@ -343,6 +355,10 @@
             now_sum = dot_at(hp[k, pl.ds(LEAD, ROWS), :], right).astype(BF)
             out_sum = dot_at(gated_s[k], grad[k + 1] if n == 0 else cot[...]).astype(BF)
             rest = HALF_ROWS - CH
+            if n == 0:
+
+                ig_send(k)
+
             for m in range(2):
                 at = 2 * n + m
                 lanes = slice(m * LANES, (m + 1) * LANES)
@@ -350,23 +366,12 @@
                 sums[k, 0, at, pl.ds(CH, rest), :] = now_sum[:rest, lanes]
                 sums[k, 1, at, pl.ds(0, CH - rest), :] = now_sum[rest:, lanes]
                 sums[k, 1, at, pl.ds(CH - rest, CH), :] = out_sum[:, lanes]
-        s1(k).start()
-
-        @pl.when(x != k)
-        def _():
-            ig_copy(k, 0).start()
-
-        @pl.when(x == k)
-        def _():
-            ig_own(k).start()
-
-        for j in range(1, GROUP):
-            ig_copy(k, j).start()
 
         @pl.when(i >= 1)
         def _():
             s1_to_s2(k + 1)
 
+        s1(k).start()
         return shift // 2
 
     lax.fori_loop(0, SECTIONS, backward, jnp.int32(BLOCK << (SECTIONS - 1)))
@@ -380,93 +385,129 @@
     skip_own.start()
     s2_to_s3(3)
     s2_to_s3(2)
-    s3_to_s4(3)
     s2_to_s3(1)
-    s3_to_s4(2)
     s2_to_s3(0)
-    s3_to_s4(1)
-    s3_to_s4(0)
-
-    total = z_s[x].astype(F32)
+
+    total = y_s[x].astype(F32)
     for j in range(1, SECTIONS):
-        s4_recv(j).wait_recv()
+        s3_recv(j).wait_recv()
         total = total + x_r[j - 1].astype(F32)
+    x_s[...] = total.astype(BF)
+    for j in range(1, ZS):
+        s4(j).start()
+    total = x_s[piece(z), :].astype(F32)
+    for j in range(1, ZS):
+        s4(j).wait_recv()
+        total = total + z_r[j - 1].astype(F32)
     full[core, y, piece(z), :] = total.astype(BF)
     for j in range(1, ZS):
         s5(j, z).start()
-    for j in range(1, ZS):
-        s5(j, lax.rem(z - j + ZS, ZS)).wait_recv()
-    for j in range(1, YS):
-        s6(j, y).start()
-    for j in range(1, YS):
-        s6(j, lax.rem(y - j + YS, YS)).wait_recv()
-    s7(core).start()
-    s7(1 - core).wait_recv()
-    scale = 1.0 / math.sqrt(SECTIONS * ROWS * SHARDS)
-    rest = HALF_ROWS - CH
-    for at in range(YS):
-        lanes = pl.ds(at * LANES, LANES)
-        out_tap[0, :, lanes] = full[0, at, pl.ds(0, CH), :].astype(F32) * scale
-        out_now[0, pl.ds(0, rest), lanes] = full[0, at, pl.ds(CH, rest), :].astype(F32) * scale
-        out_now[0, pl.ds(rest, CH - rest), lanes] = (
-            full[1, at, pl.ds(0, CH - rest), :].astype(F32) * scale
-        )
-        out = out_res if at < 2 else out_wskip
-        lanes = pl.ds(at % 2 * LANES, LANES)
-        out[0, :, lanes] = full[1, at, pl.ds(CH - rest, CH), :].astype(F32) * scale
-
+    near = (0, 1, ZS - 1, 2, ZS - 2, 3, ZS - 3, 4)
+    for j in near:
+        part = lax.rem(z - j + ZS, ZS)
+        if j:
+            s5(j, part).wait_recv()
+        for i in range(1, YS):
+            s6(i, y, part).start()
+        s7(y, part).start()
+    for j in near:
+        part = lax.rem(z - j + ZS, ZS)
+        for i in range(1, YS):
+            whose = lax.rem(y - i + YS, YS)
+            s6(i, whose, part).wait_recv()
+            s7(whose, part).start()
+    s7_all(1 - core).wait_recv()
+    done = pltpu.make_async_copy(full, out_sums, sem_loc.at[3])
+    done.start()
+
+    for copy in weights:
+        copy.wait_send()
     for n in range(3):
         others(in_ss.at[n], in_rs.at[n]).wait_send()
     others(skt_ss.at[0], skt_rs.at[0]).wait_send()
     others(ig_ss.at[x], ig_rs.at[0]).wait_recv()
     others(ig_ss.at[x], ig_rs.at[0]).wait_send()
     for j in range(1, SECTIONS):
-        w_copy(x, j).wait_send()
         skip_copy(j).wait_send()
         skip_recv(j).wait_recv()
         whole(ig_ss.at[0], ig_rs.at[j]).wait_recv()
     skip_own.wait()
     ig_own(x).wait()
     for j in range(1, ZS):
+        s4(j).wait_send()
         s5(j, z).wait_send()
     for j in range(1, YS):
-        s6(j, y).wait_send()
-    s7(core).wait_send()
+        for part in range(ZS):
+            s6(j, y, part).wait_send()
+    s7_all(core).wait_send()
 
     def drain(k, carry):
         @pl.when(x != k)
         def _():
             w_mate(k, core).wait_send()
-            s4(k).wait_send()
+            s3(k).wait_send()
             whole(ig_ss.at[k], ig_rs.at[0]).wait_send()
 
         s1(k).wait_send()
         for j in range(1, YS):
             s2(k, j).wait_send()
-        for j in range(1, ZS):
-            s3(k, j).wait_send()
         return carry
 
     lax.fori_loop(0, SECTIONS, drain, jnp.int32(0))
+    done.wait()
+
+
+def finish(
+    in_skip, in_grads, in_sums, out_skip, out_grads, out_tap, out_now, out_res, out_wskip,
+    skip, grads, sums, tap, now, res, wskip, sem_in, sem_out,
+):
+    fetch = [pltpu.make_async_copy(in_sums, sums, sem_in.at[2 * SECTIONS])]
+    store = []
+    for i in range(SECTIONS):
+        fetch.append(pltpu.make_async_copy(in_skip.at[i], skip.at[i], sem_in.at[i]))
+        store.append(pltpu.make_async_copy(skip.at[i], out_skip.at[i], sem_out.at[i]))
+        j = SECTIONS + i
+        fetch.append(pltpu.make_async_copy(in_grads.at[0, i], grads.at[i], sem_in.at[j]))
+        store.append(pltpu.make_async_copy(grads.at[i], out_grads.at[0, i], sem_out.at[j]))
+    for copy in fetch:
+        copy.start()
+    fetch[0].wait()
+    scale = 1.0 / math.sqrt(SECTIONS * ROWS * SHARDS)
+    rest = HALF_ROWS - CH
+    for at in range(YS):
+        lanes = pl.ds(at * LANES, LANES)
+        tap[:, lanes] = sums[0, at, pl.ds(0, CH), :].astype(F32) * scale
+        now[pl.ds(0, rest), lanes] = sums[0, at, pl.ds(CH, rest), :].astype(F32) * scale
+        now[pl.ds(rest, CH - rest), lanes] = (
+            sums[1, at, pl.ds(0, CH - rest), :].astype(F32) * scale
+        )
+        out = res if at < 2 else wskip
+        lanes = pl.ds(at % 2 * LANES, LANES)
+        out[:, lanes] = sums[1, at, pl.ds(CH - rest, CH), :].astype(F32) * scale
+        for i in (2 * at, 2 * at + 1):
+            fetch[1 + i].wait()
+            store[i].start()
+    pairs = ((tap, out_tap), (now, out_now), (res, out_res), (wskip, out_wskip))
+    for i, (got, to) in enumerate(pairs):
+        store.append(pltpu.make_async_copy(got, to.at[0], sem_out.at[2 * SECTIONS + i]))
+        store[-1].start()
+    for copy in store:
+        copy.wait()
 
 
 def body(signal, skip_cot, res_cot, w_tap, w_now, w_res, w_skip):
     any_space = pl.BlockSpec(memory_space=pl.ANY)
-    vmem = pl.BlockSpec(memory_space=pltpu.VMEM)
     dma = pltpu.SemaphoreType.DMA
     n = SECTIONS
-    return pl.pallas_call(
+    gathered = pl.pallas_call(
         kernel,
         out_shape=(
             jax.ShapeDtypeStruct((n, ROWS, CH), BF),
             jax.ShapeDtypeStruct((1, n, ROWS, CH), BF),
-            jax.ShapeDtypeStruct((1, CH, 2 * CH), F32),
-            jax.ShapeDtypeStruct((1, CH, 2 * CH), F32),
-            jax.ShapeDtypeStruct((1, CH, CH), F32),
-            jax.ShapeDtypeStruct((1, CH, CH), F32),
+            jax.ShapeDtypeStruct((CORES, YS, HALF_ROWS, LANES), BF),
         ),
         in_specs=[any_space] * 7,
-        out_specs=(any_space,) * 2 + (vmem,) * 4,
+        out_specs=(any_space,) * 3,
         scratch_shapes=[
             pltpu.VMEM((n, 3 * CH, 2 * CH), BF),
             pltpu.VMEM((n + 1, LEAD + ROWS, CH), BF),
@@ -486,13 +527,13 @@
             pltpu.VMEM((n, YS, HALF_ROWS, LANES), BF),
             pltpu.VMEM((n, YS - 1, HALF_ROWS, LANES), BF),
             pltpu.VMEM((n, HALF_ROWS, LANES), BF),
-            pltpu.VMEM((n, ZS - 1, PIECE, LANES), BF),
-            pltpu.VMEM((n, PIECE, LANES), BF),
-            pltpu.VMEM((n - 1, PIECE, LANES), BF),
+            pltpu.VMEM((n - 1, HALF_ROWS, LANES), BF),
+            pltpu.VMEM((HALF_ROWS, LANES), BF),
+            pltpu.VMEM((ZS - 1, PIECE, LANES), BF),
             pltpu.VMEM((CORES, YS, HALF_ROWS, LANES), BF),
             dma((7,)),
-            dma((3,)),
-            dma((n - 1,)), dma((n - 1,)),
+            dma((4,)),
+            dma((6,)), dma((2 * n,)),
             dma((n,)), dma((n,)),
             dma((3,)), dma((3,)),
             dma((1,)), dma((1,)),
@@ -500,16 +541,42 @@
             dma((n,)), dma((n,)),
             dma((n,)), dma((n,)),
             dma((n * (YS - 1),)), dma((n * (YS - 1),)),
-            dma((n * (ZS - 1),)), dma((n * (ZS - 1),)),
             dma((n,)), dma((n - 1,)),
             dma((ZS - 1,)), dma((ZS - 1,)),
-            dma((YS - 1,)), dma((YS - 1,)),
+            dma((ZS - 1,)), dma((ZS - 1,)),
+            dma(((YS - 1) * ZS,)), dma(((YS - 1) * ZS,)),
             dma((1,)), dma((1,)),
+            pltpu.SemaphoreType.REGULAR,
         ],
         compiler_params=pltpu.CompilerParams(
             collective_id=0, has_side_effects=True, vmem_limit_bytes=56 << 20
         ),
     )(signal, skip_cot, res_cot, w_tap, w_now, w_res, w_skip)
+    return pl.pallas_call(
+        finish,
+        out_shape=(
+            jax.ShapeDtypeStruct((n, ROWS, CH), BF),
+            jax.ShapeDtypeStruct((1, n, ROWS, CH), BF),
+            jax.ShapeDtypeStruct((1, CH, 2 * CH), F32),
+            jax.ShapeDtypeStruct((1, CH, 2 * CH), F32),
+            jax.ShapeDtypeStruct((1, CH, CH), F32),
+            jax.ShapeDtypeStruct((1, CH, CH), F32),
+        ),
+        in_specs=[any_space] * 3,
+        out_specs=(any_space,) * 6,
+        scratch_shapes=[
+            pltpu.VMEM((n, ROWS, CH), BF),
+            pltpu.VMEM((n, ROWS, CH), BF),
+            pltpu.VMEM((CORES, YS, HALF_ROWS, LANES), BF),
+            pltpu.VMEM((CH, 2 * CH), F32),
+            pltpu.VMEM((CH, 2 * CH), F32),
+            pltpu.VMEM((CH, CH), F32),
+            pltpu.VMEM((CH, CH), F32),
+            dma((2 * n + 1,)),
+            dma((2 * n + 4,)),
+        ],
+        compiler_params=pltpu.CompilerParams(vmem_limit_bytes=56 << 20),
+    )(*gathered)
 
 
 def solution(mesh):

time: 105 us -> 94.1 us (0.90)
  local copies, waits for them, and re-layouts: 7.82 us -> 0 us
  Pallas kernels: 96.3 us -> 93.3 us
    unnamed x16 -> x0, local copies, waits for them, and re-layouts: 7.82 us -> none
    pallas_call x1, Pallas kernels: 96.3 us -> 90.1 us  [body(): pl.pallas_call(kernel, out_shape=(jax.ShapeDtypeStruct((n, ROWS, CH), BF)...]
    pallas_call x0 -> x1, Pallas kernels: none -> 3.19 us  [body(): pl.pallas_call(finish, out_shape=(jax.ShapeDtypeStruct((n, ROWS, CH), BF)...]
where the time goes in v3:
time: 94.1 us; the launch traced here: 94 us
  Pallas kernels  93.3 us (99%)
    pallas_call x1, Pallas kernels, body(): pl.pallas_call(kernel, out_shape=(jax.ShapeDtypeStruct((n, ROWS, CH), BF)...  90.1 us
    pallas_call x1, Pallas kernels, body(): pl.pallas_call(finish, out_shape=(jax.ShapeDtypeStruct((n, ROWS, CH), BF)...  3.19 us

profile of v3, /device:TPU:1, one launch (start us, length us, event | category | flops | bytes accessed | tf_op | source)
XLA Modules:
  0.0 94.0 jit_solution(12032172227184203781)
XLA Ops:
  0.6 90.1 %shard_map.118 = (bf16[4,512,256]{2,1,0:T(8,128)(2,1)}, bf16[1,4,512,256]{3,2,1,0:T(8,128)(2,1)}, bf16[2,4,384,128]{3,2,1,0:T(8,128)(2,1)}) custom-call(bf16[4,512,256]{2,1,0:T(8,128)(2,1)} %signal.1, bf16[4,512,256]{2,1,0:T(8,128)(2,1)} %skip_cot.1, bf16[4,512,256]{2,1,0:T(8,128)(2,1)} %res_cot.1, bf16[1,256,512]{2,1,0:T(8,128)(2,1)} %w_tap.1, ...), custom_call_target="tpu_custom_call" | custom-call | tf_op jit(solution)/shard_map/pallas_call | solution.py:502
  90.8 3.2 %shard_map.119 = (bf16[4,512,256]{2,1,0:T(8,128)(2,1)}, bf16[1,4,512,256]{3,2,1,0:T(8,128)(2,1)}, f32[1,256,512]{2,1,0:T(8,128)}, f32[1,256,512]{2,1,0:T(8,128)}...) custom-call(bf16[4,512,256]{2,1,0:T(8,128)(2,1)} %get-tuple-element.9.in_skip, ...), custom_call_target="tpu_custom_call" | custom-call | tf_op jit(solution)/shard_map/pallas_call | solution.py:555

commit v4 on v3

--- a/solution.py
+++ b/solution.py
@@ -16,6 +16,7 @@
 SHARDS = YS * ZS * CORES
 ROWS, CH = 512, 256
 GROUP = 16
+ORDER = (1, 3, 4, 12, 5, 15, 7, 13, 2, 8, 9, 11, 6, 14, 10)
 BLOCK = ROWS // GROUP
 LEAD = ROWS // 2
 PARTS = 2
@@ -41,7 +42,7 @@
     signal, skip_cot, res_cot, w_tap, w_now, w_res, w_skip,
     out_skip, out_grads, out_sums,
     wts, hp, act, sig, gated_s, skip_acc, skip_out, skip_t, cot, grad, dz, bp, part_g,
-    sums, pair_r, pair_s, y_r, y_s, x_r, x_s, z_r, full,
+    sums, pair_r, pair_s, y_r, y_s, z_r, z_s, x_r, full,
     sem_in, sem_loc, w_ss, w_rs, wp_ss, wp_rs, in_ss, in_rs,
     skt_ss, skt_rs, skip_ss, skip_rs, ig_ss, ig_rs, s1_ss, s1_rs, s2_ss, s2_rs, s3_ss, s3_rs,
     s4_ss, s4_rs, s5_ss, s5_rs, s6_ss, s6_rs, s7_ss, s7_rs, ready,
@@ -168,20 +169,20 @@
     def piece(i):
         return pl.ds(pl.multiple_of(i * PIECE, 16), PIECE)
 
-    def s3(layer):
+    def s3(layer, j):
+        return remote(
+            y_s.at[layer, piece(lax.rem(z + j, ZS))], z_r.at[layer, j - 1],
+            s3_ss.at[layer * 7 + j - 1], s3_rs.at[layer * 7 + j - 1], x, at_z(j),
+        )
+
+    def s4(layer):
         j = lax.rem(layer - x + SECTIONS, SECTIONS)
         return remote(
-            y_s.at[layer], x_r.at[j - 1], s3_ss.at[layer], s3_rs.at[j - 1], layer, t
-        )
-
-    def s3_recv(j):
-        return remote(y_s.at[0], x_r.at[j - 1], s3_ss.at[0], s3_rs.at[j - 1], at_x(-j), t)
-
-    def s4(j):
-        return remote(
-            x_s.at[piece(lax.rem(z + j, ZS))], z_r.at[j - 1],
-            s4_ss.at[j - 1], s4_rs.at[j - 1], x, at_z(j),
-        )
+            z_s.at[layer], x_r.at[j - 1], s4_ss.at[layer], s4_rs.at[j - 1], layer, t
+        )
+
+    def s4_recv(j):
+        return remote(z_s.at[0], x_r.at[j - 1], s4_ss.at[0], s4_rs.at[j - 1], at_x(-j), t)
 
     def s5(j, whose):
         return remote(
@@ -216,7 +217,7 @@
 
     barrier = pltpu.get_barrier_semaphore()
     peers = [(x, mate)] + [(x, at_z(j)) for j in (1, 3, 5, 7)]
-    peers += [(x, member(j)[1]) for j in range(1, GROUP)]
+    peers += [(x, member(j)[1]) for j in ORDER]
     peers += [(at_x(j), t) for j in range(1, SECTIONS)]
     for peer in peers:
         pl.semaphore_signal(barrier, inc=1, device_id=peer, device_id_type=MESH)
@@ -229,7 +230,7 @@
     for j in range(1, SECTIONS):
         pl.semaphore_signal(ready, inc=1, device_id=(at_x(j), t), device_id_type=MESH)
 
-    for j in range(1, GROUP):
+    for j in ORDER:
         spread(0, j).start()
     for load in loads[:4]:
         load.wait()
@@ -237,7 +238,7 @@
     for copy in weights[:4]:
         copy.start()
     for n in (1, 2):
-        for j in range(1, GROUP):
+        for j in ORDER:
             spread(n, j).start()
 
     left, right, across = at_x(-1), at_x(1), at_x(2)
@@ -284,6 +285,12 @@
     lax.fori_loop(0, SECTIONS, forward, jnp.int32(BLOCK))
 
     skip_out[...] = skip_acc[...].astype(BF)
+    for j in ORDER:
+        skip_back(j).start()
+    skip_mine = pltpu.make_async_copy(
+        skip_out.at[block(me)], skip_t.at[block(me)], sem_loc.at[1]
+    )
+    skip_mine.start()
 
     def s1_to_s2(layer):
         s1(layer).wait_recv()
@@ -299,32 +306,23 @@
             s2(layer, j).wait_recv()
             total = total + y_r[layer, j - 1].astype(F32)
         y_s[layer] = total.astype(BF)
+        for j in range(1, ZS):
+            s3(layer, j).start()
+
+    def s3_to_s4(layer):
+        total = y_s[layer, piece(z), :].astype(F32)
+        for j in range(1, ZS):
+            s3(layer, j).wait_recv()
+            total = total + z_r[layer, j - 1].astype(F32)
+        z_s[layer] = total.astype(BF)
 
         @pl.when(x != layer)
         def _():
-            s3(layer).start()
-
-    def ig_send(layer):
-        @pl.when(x != layer)
-        def _():
-            ig_copy(layer, 0).start()
-
-        @pl.when(x == layer)
-        def _():
-            ig_own(layer).start()
-
-        for j in range(1, GROUP):
-            ig_copy(layer, j).start()
+            s4(layer).start()
 
     for n in (1, 2):
         loads[4 + n].wait()
         others(in_ss.at[n], in_rs.at[n]).wait_recv()
-    for j in range(1, GROUP):
-        skip_back(j).start()
-    skip_mine = pltpu.make_async_copy(
-        skip_out.at[block(me)], skip_t.at[block(me)], sem_loc.at[1]
-    )
-    skip_mine.start()
     pl.semaphore_wait(ready, SECTIONS - 1)
 
     def backward(i, shift):
@@ -356,8 +354,16 @@
             out_sum = dot_at(gated_s[k], grad[k + 1] if n == 0 else cot[...]).astype(BF)
             rest = HALF_ROWS - CH
             if n == 0:
-
-                ig_send(k)
+                @pl.when(x != k)
+                def _():
+                    ig_copy(k, 0).start()
+
+                @pl.when(x == k)
+                def _():
+                    ig_own(k).start()
+
+                for j in ORDER:
+                    ig_copy(k, j).start()
 
             for m in range(2):
                 at = 2 * n + m
@@ -366,12 +372,12 @@
                 sums[k, 0, at, pl.ds(CH, rest), :] = now_sum[:rest, lanes]
                 sums[k, 1, at, pl.ds(0, CH - rest), :] = now_sum[rest:, lanes]
                 sums[k, 1, at, pl.ds(CH - rest, CH), :] = out_sum[:, lanes]
+        s1(k).start()
 
         @pl.when(i >= 1)
         def _():
             s1_to_s2(k + 1)
 
-        s1(k).start()
         return shift // 2
 
     lax.fori_loop(0, SECTIONS, backward, jnp.int32(BLOCK << (SECTIONS - 1)))
@@ -385,20 +391,17 @@
     skip_own.start()
     s2_to_s3(3)
     s2_to_s3(2)
+    s3_to_s4(3)
     s2_to_s3(1)
+    s3_to_s4(2)
     s2_to_s3(0)
-
-    total = y_s[x].astype(F32)
+    s3_to_s4(1)
+    s3_to_s4(0)
+
+    total = z_s[x].astype(F32)
     for j in range(1, SECTIONS):
-        s3_recv(j).wait_recv()
+        s4_recv(j).wait_recv()
         total = total + x_r[j - 1].astype(F32)
-    x_s[...] = total.astype(BF)
-    for j in range(1, ZS):
-        s4(j).start()
-    total = x_s[piece(z), :].astype(F32)
-    for j in range(1, ZS):
-        s4(j).wait_recv()
-        total = total + z_r[j - 1].astype(F32)
     full[core, y, piece(z), :] = total.astype(BF)
     for j in range(1, ZS):
         s5(j, z).start()
@@ -434,7 +437,6 @@
     skip_own.wait()
     ig_own(x).wait()
     for j in range(1, ZS):
-        s4(j).wait_send()
         s5(j, z).wait_send()
     for j in range(1, YS):
         for part in range(ZS):
@@ -445,12 +447,14 @@
         @pl.when(x != k)
         def _():
             w_mate(k, core).wait_send()
-            s3(k).wait_send()
+            s4(k).wait_send()
             whole(ig_ss.at[k], ig_rs.at[0]).wait_send()
 
         s1(k).wait_send()
         for j in range(1, YS):
             s2(k, j).wait_send()
+        for j in range(1, ZS):
+            s3(k, j).wait_send()
         return carry
 
     lax.fori_loop(0, SECTIONS, drain, jnp.int32(0))
@@ -527,9 +531,9 @@
             pltpu.VMEM((n, YS, HALF_ROWS, LANES), BF),
             pltpu.VMEM((n, YS - 1, HALF_ROWS, LANES), BF),
             pltpu.VMEM((n, HALF_ROWS, LANES), BF),
-            pltpu.VMEM((n - 1, HALF_ROWS, LANES), BF),
-            pltpu.VMEM((HALF_ROWS, LANES), BF),
-            pltpu.VMEM((ZS - 1, PIECE, LANES), BF),
+            pltpu.VMEM((n, ZS - 1, PIECE, LANES), BF),
+            pltpu.VMEM((n, PIECE, LANES), BF),
+            pltpu.VMEM((n - 1, PIECE, LANES), BF),
             pltpu.VMEM((CORES, YS, HALF_ROWS, LANES), BF),
             dma((7,)),
             dma((4,)),
@@ -541,8 +545,8 @@
             dma((n,)), dma((n,)),
             dma((n,)), dma((n,)),
             dma((n * (YS - 1),)), dma((n * (YS - 1),)),
+            dma((n * (ZS - 1),)), dma((n * (ZS - 1),)),
             dma((n,)), dma((n - 1,)),
-            dma((ZS - 1,)), dma((ZS - 1,)),
             dma((ZS - 1,)), dma((ZS - 1,)),
             dma(((YS - 1) * ZS,)), dma(((YS - 1) * ZS,)),
             dma((1,)), dma((1,)),

time: 94.1 us -> 93.1 us (0.989)
    pallas_call x1, Pallas kernels: 90.1 us -> 89.2 us  [body(): pl.pallas_call(kernel, out_shape=(jax.ShapeDtypeStruct((n, ROWS, CH), BF)...]
where the time goes in v4:
time: 93.1 us; the launch traced here: 93 us
  Pallas kernels  92.4 us (99%)
    pallas_call x1, Pallas kernels, body(): pl.pallas_call(kernel, out_shape=(jax.ShapeDtypeStruct((n, ROWS, CH), BF)...  89.2 us
    pallas_call x1, Pallas kernels, body(): pl.pallas_call(finish, out_shape=(jax.ShapeDtypeStruct((n, ROWS, CH), BF)...  3.19 us

profile of v4, /device:TPU:1, one launch (start us, length us, event | category | flops | bytes accessed | tf_op | source)
XLA Modules:
  0.0 93.0 jit_solution(11542907961702700665)
XLA Ops:
  0.6 89.2 %shard_map.118 = (bf16[4,512,256]{2,1,0:T(8,128)(2,1)}, bf16[1,4,512,256]{3,2,1,0:T(8,128)(2,1)}, bf16[2,4,384,128]{3,2,1,0:T(8,128)(2,1)}) custom-call(bf16[4,512,256]{2,1,0:T(8,128)(2,1)} %signal.1, bf16[4,512,256]{2,1,0:T(8,128)(2,1)} %skip_cot.1, bf16[4,512,256]{2,1,0:T(8,128)(2,1)} %res_cot.1, bf16[1,256,512]{2,1,0:T(8,128)(2,1)} %w_tap.1, ...), custom_call_target="tpu_custom_call" | custom-call | tf_op jit(solution)/shard_map/pallas_call | solution.py:506
  89.8 3.2 %shard_map.119 = (bf16[4,512,256]{2,1,0:T(8,128)(2,1)}, bf16[1,4,512,256]{3,2,1,0:T(8,128)(2,1)}, f32[1,256,512]{2,1,0:T(8,128)}, f32[1,256,512]{2,1,0:T(8,128)}...) custom-call(bf16[4,512,256]{2,1,0:T(8,128)(2,1)} %get-tuple-element.9.in_skip, ...), custom_call_target="tpu_custom_call" | custom-call | tf_op jit(solution)/shard_map/pallas_call | solution.py:559
